TPU v7x, 128 devices: a whole 4x4x4 slice. The times are simulated.
128 devices in a mesh: freq: 4 (over z_hi, core), vis: 32 (over z_lo, y, x).
Axes of the slice: x: 4, y: 4, z: 4 (z_hi: 2, z_lo: 2; z = z_hi * 2 + z_lo), core: 2. Of those that a mesh axis runs over, the one named last changes fastest.
Arguments:
- model_input: bfloat16 [2, 16, 512, 512], P(None, 'freq', 'vis'), parts along dimension 1, may hold values from -6 to 6
- w_kernels: bfloat16 [64, 2, 128, 128], P('freq'), parts along dimension 0, may hold values from -0.375 to 0.375
- visibilities: bfloat16 [4096, 2, 128, 128], P(('freq', 'vis')), parts along dimension 0, may hold values from -6 to 6
- tile_facet: int32 [4096], P(('freq', 'vis')), parts along dimension 0, may hold values from 0 to 3
- tile_patch: int32 [4096], P(('freq', 'vis')), parts along dimension 0, may hold values from 0 to 15
- tile_wplane: int32 [4096], P(('freq', 'vis')), parts along dimension 0, may hold values from 0 to 15
- tile_count: int32 [128], P(('freq', 'vis')), parts along dimension 0, may hold values from 16 to 32, as said below
Outputs:
- residual_image: float32 [16, 512, 512], P('freq', 'vis'), parts along dimension 0
There are 4 independent parts, one for each index of `freq`. A program takes and returns all parts, laid end to end along the dimension named above; each array names one. Nothing has to cross between parts.
Inputs may be any that keep to these rules, and one draw needn't show every extreme that they name: `tile_count`: each device's live tiles fill its first slots; some device holds exactly 32.
All inputs are finite; a program needn't handle non-finite values.
Results may differ from a plain program's by a relative error of at most 0.02.
Values may be sent and summed in bfloat16 or wider, within the bound.
A program may use at most 128 MiB of HBM per device.

v0:
```python
import math

import jax
import jax.numpy as jnp
from jax import lax
from jax.sharding import PartitionSpec as P

P_SIZE = 512
S = 128
F = 4
WPLANES = 16
CYCLES = 2
TILE_CAP = 32
NP = 16


loop_gain = 0.5


def dft_tables(first_row, row_count, length):
    row_ids = first_row + jnp.arange(row_count, dtype=jnp.int32)
    col_ids = jnp.arange(length, dtype=jnp.int32)
    phases = row_ids[:, None] * col_ids[None, :] % length
    angles = phases.astype(jnp.float32) * (2.0 * math.pi / length)
    scaling = 1.0 / math.sqrt(length)
    return (jnp.cos(angles) * scaling, jnp.sin(angles) * scaling)


def lowprec(pattern, first_op, second_op):
    return jnp.einsum(pattern, first_op, second_op, preferred_element_type=jnp.float32)


def exact(pattern, first_op, second_op):
    return jnp.einsum(
        pattern,
        first_op,
        second_op,
        precision=lax.Precision.HIGHEST,
        preferred_element_type=jnp.float32,
    )


def column_pass(half_grid, cosine_half, sine_half):
    half_real, half_imag = (half_grid[:, 0], half_grid[:, 1])
    grid_real = lowprec("ij,fjk->fik", cosine_half, half_real) + lowprec(
        "ij,fjk->fik", sine_half, half_imag
    )
    grid_imag = lowprec("ij,fjk->fik", cosine_half, half_imag) - lowprec(
        "ij,fjk->fik", sine_half, half_real
    )
    return jnp.stack([grid_real, grid_imag], axis=1).astype(jnp.bfloat16)


def tile_terms(patches, kernel, observed, alive):
    patch_real, patch_imag = (patches[:, 0], patches[:, 1])
    kern_real, kern_imag = (kernel[:, 0], kernel[:, 1])
    mid_real = (
        lowprec("tij,tjk->tik", kern_real, patch_real)
        - lowprec("tij,tjk->tik", kern_imag, patch_imag)
    ).astype(jnp.bfloat16)
    mid_imag = (
        lowprec("tij,tjk->tik", kern_real, patch_imag)
        + lowprec("tij,tjk->tik", kern_imag, patch_real)
    ).astype(jnp.bfloat16)
    model_real = lowprec("tij,tkj->tik", mid_real, kern_real) - lowprec(
        "tij,tkj->tik", mid_imag, kern_imag
    )
    model_imag = lowprec("tij,tkj->tik", mid_real, kern_imag) + lowprec(
        "tij,tkj->tik", mid_imag, kern_real
    )
    resid_real = ((observed[:, 0].astype(jnp.float32) - model_real) * alive[:, None, None]).astype(
        jnp.bfloat16
    )
    resid_imag = ((observed[:, 1].astype(jnp.float32) - model_imag) * alive[:, None, None]).astype(
        jnp.bfloat16
    )
    back_real = (
        lowprec("tji,tjk->tik", kern_real, resid_real)
        + lowprec("tji,tjk->tik", kern_imag, resid_imag)
    ).astype(jnp.bfloat16)
    back_imag = (
        lowprec("tji,tjk->tik", kern_real, resid_imag)
        - lowprec("tji,tjk->tik", kern_imag, resid_real)
    ).astype(jnp.bfloat16)
    out_real = lowprec("tij,tjk->tik", back_real, kern_real) + lowprec(
        "tij,tjk->tik", back_imag, kern_imag
    )
    out_imag = lowprec("tij,tjk->tik", back_imag, kern_real) - lowprec(
        "tij,tjk->tik", back_real, kern_imag
    )
    return jnp.stack([out_real, out_imag], axis=1).reshape(patches.shape[0], 2 * S * S)


def local(model_input, w_kernels, visibilities, tile_facet, tile_patch, tile_wplane, tile_count):
    devices = lax.axis_size("vis")
    position = lax.axis_index("vis")
    local_rows = P_SIZE // devices
    cosine_full, sine_full = dft_tables(0, P_SIZE, P_SIZE)
    cosine_half = cosine_full.astype(jnp.bfloat16)
    sine_half = sine_full.astype(jnp.bfloat16)
    weight = math.sqrt(F * NP / (TILE_CAP * devices))
    slots = tile_facet * NP + tile_patch
    alive = (jnp.arange(TILE_CAP, dtype=jnp.int32) < tile_count[0]).astype(jnp.float32)
    kernel_table = w_kernels.reshape(WPLANES, 2 * S * S)
    block_count = TILE_CAP // 16
    blocks = (
        slots.reshape(block_count, 16),
        tile_wplane.reshape(block_count, 16),
        visibilities.reshape(block_count, 16, 2, S, S),
        alive.reshape(block_count, 16),
    )
    residual_image = jnp.zeros((F, local_rows, P_SIZE), jnp.float32)
    for cycle_index in range(CYCLES):
        if cycle_index == 0:
            sky_model = model_input[0]
        else:
            sky_model = (
                model_input[cycle_index].astype(jnp.float32) + loop_gain * residual_image
            ).astype(jnp.bfloat16)
        half_real = lowprec("fij,jk->fik", sky_model, cosine_half)
        half_imag = -lowprec("fij,jk->fik", sky_model, sine_half)
        half_grid = jnp.stack([half_real, half_imag], axis=1).astype(jnp.bfloat16)
        column_half = lax.all_to_all(half_grid, "vis", split_axis=3, concat_axis=2, tiled=True)
        grid_part = column_pass(column_half, cosine_half, sine_half)
        full_grid = lax.all_gather(grid_part, "vis", axis=3, tiled=True)
        patch_table = (
            full_grid.reshape(F, 2, P_SIZE // S, S, P_SIZE // S, S)
            .transpose(0, 2, 4, 1, 3, 5)
            .reshape(F * NP, 2 * S * S)
        )

        def accumulate(running, tile_block):
            slot_ids, plane_ids, observed, live_block = tile_block
            choose = (slot_ids[:, None] == jnp.arange(F * NP, dtype=jnp.int32)[None, :]).astype(
                jnp.bfloat16
            )
            patches = (
                jnp.dot(choose, patch_table, preferred_element_type=jnp.float32)
                .astype(jnp.bfloat16)
                .reshape(16, 2, S, S)
            )
            plane_pick = (
                plane_ids[:, None] == jnp.arange(WPLANES, dtype=jnp.int32)[None, :]
            ).astype(jnp.bfloat16)
            kernel = (
                jnp.dot(plane_pick, kernel_table, preferred_element_type=jnp.float32)
                .astype(jnp.bfloat16)
                .reshape(16, 2, S, S)
            )
            tile_sums = tile_terms(patches, kernel, observed, live_block)
            return (running.at[slot_ids].add(tile_sums), None)

        summed, unused = lax.scan(accumulate, jnp.zeros((F * NP, 2 * S * S), jnp.float32), blocks)
        resid_grid = (
            summed.reshape(F, P_SIZE // S, P_SIZE // S, 2, S, S)
            .transpose(0, 3, 1, 4, 2, 5)
            .reshape(F, 2, P_SIZE, P_SIZE)
        )
        total_grid = lax.psum(resid_grid.astype(jnp.bfloat16), "vis").astype(jnp.float32)
        cosine_rows, sine_rows = dft_tables(position * local_rows, local_rows, P_SIZE)
        spec_real = exact("ij,fjk->fik", cosine_rows, total_grid[:, 0]) - exact(
            "ij,fjk->fik", sine_rows, total_grid[:, 1]
        )
        spec_imag = exact("ij,fjk->fik", cosine_rows, total_grid[:, 1]) + exact(
            "ij,fjk->fik", sine_rows, total_grid[:, 0]
        )
        residual_image = (
            exact("fij,jk->fik", spec_real, cosine_full)
            - exact("fij,jk->fik", spec_imag, sine_full)
        ) * weight
    return residual_image


def solution(mesh):
    return jax.shard_map(
        local,
        mesh=mesh,
        in_specs=(
            P(None, "freq", "vis", None),
            P("freq", None, None, None),
            P(("freq", "vis"), None, None, None),
            P(("freq", "vis")),
            P(("freq", "vis")),
            P(("freq", "vis")),
            P(("freq", "vis")),
        ),
        out_specs=P("freq", "vis", None),
        check_vma=False,
    )
```

profile of v0, /device:TPU:0, one launch (start us, length us, event | category | flops | bytes accessed | tf_op | source)
XLA Modules:
  0.0 1282.2 jit_solution(3081509541282992001)
XLA Ops:
  6.5 5.0 fusion.92
  17.6 17.2 %all_to_all.36 = bf16[32,2,1024]{2,1,0:T(2,128)(2,1)S(1)} all-to-all(bf16[32,2,1024]{2,1,0:T(2,128)(2,1)S(1)} %reshape.173), channel_id=1, replica_groups=mesh['freq'=4,'vis'=32] {'vis'}, dimensions={0} | all-to-all | bytes 262144 | tf_op jit(solution)/shard_map/all_to_all | solution.py:123
  59.6 152.0 %all-gather.3.cloned.1.call-done = bf16[4,2,512,512]{2,3,0,1:T(8,128)(2,1)} async-done(((bf16[4,2,512,16]{2,3,0,1:T(8,128)(2,1)}), bf16[4,2,512,512]{2,3,0,1:T(8,128)(2,1)}) %all-gather.3.cloned.1.call-update) | async-done | bytes 4194320 | tf_op jit(solution)/shard_map/all_gather | solution.py:125
  211.6 7.0 reshape.138
  218.5 7.5 copy.83
  226.0 7.3 reshape.139
  237.2 43.1 %while.20 = (s32[]{:T(128)}, f32[64,32768]{1,0:T(8,128)}, s32[2,16]{1,0:T(2,128)S(1)}, s32[2,16]{1,0:T(2,128)S(1)}, bf16[16,32768]{1,0:T(8,128)(2,1)S(1)}, /*ind...) while((s32[]{:T(128)}, f32[64,32768]{1,0:T(8,128)}, ...), condition=%wide.region_2.3_spmd, body=%wide.region_0.2_spmd.sunk | while | flops 1164969216 | bytes 89130760 | solution.py:153
  248.0 10.6 scatter_custom_fusion.9
  269.4 10.6 scatter_custom_fusion.9
  285.6 5.9 copy.143
  291.5 7.2 convert_element_type.191
  303.2 321.4 %all-reduce.3.cloned.1.call-done = bf16[4,2,512,512]{3,2,0,1:T(8,128)(2,1)} async-done(((bf16[4,2,512,512]{3,2,0,1:T(8,128)(2,1)}), bf16[4,2,512,512]{3,2,0,1:T(8,128)(2,1)}) %all-reduce.3.cloned.1.call-update) | async-done | bytes 4194320 | tf_op jit(solution)/shard_map/psum | solution.py:159
  652.7 15.9 %all_to_all.37 = bf16[32,2,1024]{2,1,0:T(2,128)(2,1)S(1)} all-to-all(bf16[32,2,1024]{2,1,0:T(2,128)(2,1)S(1)} %reshape.175), channel_id=1, replica_groups=mesh['freq'=4,'vis'=32] {'vis'}, dimensions={0} | all-to-all | bytes 262144 | tf_op jit(solution)/shard_map/all_to_all | solution.py:123
  689.0 155.5 %all-gather.5.cloned.1.call-done = bf16[4,2,512,512]{2,3,0,1:T(8,128)(2,1)} async-done(((bf16[4,2,512,16]{2,3,0,1:T(8,128)(2,1)}), bf16[4,2,512,512]{2,3,0,1:T(8,128)(2,1)}) %all-gather.5.cloned.1.call-update) | async-done | bytes 4194320 | tf_op jit(solution)/shard_map/all_gather | solution.py:125
  844.4 7.1 reshape.140
  851.5 7.5 copy.92
  859.0 7.3 reshape.141
  870.2 42.9 %while.21 = (s32[]{:T(128)}, f32[64,32768]{1,0:T(8,128)}, s32[2,16]{1,0:T(2,128)S(1)}, s32[2,16]{1,0:T(2,128)S(1)}, bf16[16,32768]{1,0:T(8,128)(2,1)S(1)}, /*ind...) while((s32[]{:T(128)}, f32[64,32768]{1,0:T(8,128)}, ...), condition=%wide.region_6.7_spmd, body=%wide.region_4.6_spmd.sunk | while | flops 1164969216 | bytes 89130760 | solution.py:153
  881.0 10.6 scatter_custom_fusion.11
  902.3 10.6 scatter_custom_fusion.11
  918.3 5.9 copy.142
  924.2 7.2 convert_element_type.197
  935.9 321.6 %all-reduce.5.cloned.1.call-done = bf16[4,2,512,512]{3,2,0,1:T(8,128)(2,1)} async-done(((bf16[4,2,512,512]{3,2,0,1:T(8,128)(2,1)}), bf16[4,2,512,512]{3,2,0,1:T(8,128)(2,1)}) %all-reduce.5.cloned.1.call-update) | async-done | bytes 4194320 | tf_op jit(solution)/shard_map/psum | solution.py:159
  1269.8 5.6 fusion.72
  (185 shorter events, 160.4 us)
Async XLA Ops:
  6.5 5.1 copy-start.5
  6.5 205.0 %all-gather.3.cloned.1.call-start = ((), (), s32[]{:S(2)}) async-start(), calls=%async_computation.2 | async-start | bytes 4325376 | tf_op jit(solution)/shard_map/all_gather | solution.py:125
  46.0 9.4 copy-start.4
  54.6 4.8 copy-start.6
  54.6 4.8 copy-start.7
  54.6 4.9 copy-start.8
  55.3 569.2 %all-reduce.3.cloned.1.call-start = ((), (), s32[]{:S(2)}) async-start(), calls=%async_computation.3 | async-start | bytes 8388608 | tf_op jit(solution)/shard_map/psum | solution.py:159
  237.2 2.2 copy-start.1
  258.6 2.2 copy-start.1
  303.1 541.3 %all-gather.5.cloned.1.call-start = ((), (), s32[]{:S(2)}) async-start(), calls=%async_computation.4 | async-start | bytes 4325376 | tf_op jit(solution)/shard_map/all_gather | solution.py:125
  624.6 10.4 copy-start.2
  688.9 568.6 %all-reduce.5.cloned.1.call-start = ((), (), s32[]{:S(2)}) async-start(), calls=%async_computation.5 | async-start | bytes 8388608 | tf_op jit(solution)/shard_map/psum | solution.py:159
  870.2 2.2 copy-start
  891.6 2.2 copy-start
  1257.5 10.2 copy-start.3
Sparse Core Ops, SparseCore 0:
  55.4 156.0 all-gather.2
  303.2 321.2 all-reduce.2
  689.0 155.3 all-gather.4
  936.0 321.3 all-reduce.4
where the time goes:
time: 1290 us; the launch traced here: 1280 us
  waiting for transfers between devices  950 us (74%)
  local copies, waits for them, and re-layouts  116 us (9%)
  matrix products  114 us (9%)
  other arithmetic  52.7 us (4%)
  blocking collectives  33.1 us (3%)
  between operations  14.4 us (1%)
    psum x2, waiting for transfers between devices, local(): lax.psum(resid_grid.astype(jnp.bfloat16), 'vis').astype(jnp.float32)  643 us
    all_gather x2, waiting for transfers between devices, local(): full_grid = lax.all_gather(grid_part, 'vis', axis=3, tiled=True)  307 us
    dot_general x76, matrix products, lowprec(): jnp.einsum(pattern, first_op, second_op, preferred_element_type=jnp.float32)  74.3 us
    scatter-add x4, other arithmetic, accumulate(): return (running.at[slot_ids].add(tile_sums), None)  42.3 us
    dot_general x12, matrix products, exact(): jnp.einsum(pattern, first_op, second_op, precision=lax.Precision.HIGHEST,...  35.2 us
    convert_element_type x6, local copies, waits for them, and re-layouts, local(): resid_grid.astype(jnp.bfloat16)  35.1 us
    all_to_all x2, blocking collectives, local(): lax.all_to_all(half_grid, 'vis', split_axis=3, concat_axis=2, tiled=True)  33.1 us
  transfers between devices with their start and end apart: 4, of which 4 were waited for; matrix products, arithmetic and copies ran while one was open for 0% of the time, Pallas kernels for 0%

commit v1 on v0

v1 whole, which is shorter than its diff:
```python
import functools
import math

import jax
import jax.numpy as jnp
import numpy as np
from jax import lax
from jax.experimental import pallas as pl
from jax.experimental.pallas import tpu as pltpu
from jax.sharding import PartitionSpec as P

P_SIZE = 512
S = 128
F = 4
WPLANES = 16
TILE_CAP = 32
NP = 16
SLOTS = F * NP
DEVICES = 32
ROWS = P_SIZE // DEVICES
TILES = TILE_CAP * DEVICES
WEIGHT = math.sqrt(F * NP / TILES)
LOOP_GAIN = 0.5
MESH = pl.DeviceIdType.MESH
BF16 = jnp.bfloat16
F32 = jnp.float32
VIS_CHUNK = 4


def dot(a, b):
    return lax.dot_general(a, b, (((1,), (0,)), ((), ())), preferred_element_type=F32)


def lanes(*parts):
    return jnp.concatenate(parts, axis=1)


def stack(*parts):
    return jnp.concatenate(parts, axis=0)


def regrid_kernel(
    facet_ref, patch_ref, plane_ref, count_ref, w_ref, vis_hbm, grid_ref, cnt_ref,
    vis_buf, back_op, term_op, acc, cnt_acc, sems,
):
    copies = [
        pltpu.make_async_copy(
            vis_hbm.at[pl.ds(k * VIS_CHUNK, VIS_CHUNK)],
            vis_buf.at[pl.ds(k * VIS_CHUNK, VIS_CHUNK)],
            sems.at[k],
        )
        for k in range(TILE_CAP // VIS_CHUNK)
    ]
    for copy in copies:
        copy.start()

    @pl.loop(0, WPLANES)
    def _(w):
        real, imag = w_ref[w, 0], w_ref[w, 1]
        back_op[w] = lanes(real.T, imag.T)
        term_op[w] = stack(lanes(real, -imag), lanes(imag, real))

    @pl.loop(0, SLOTS + 1)
    def _(s):
        acc[s] = jnp.zeros((S, 2 * S), F32)
        cnt_acc[s] = jnp.zeros((WPLANES, S), F32)

    for k, copy in enumerate(copies):
        copy.wait()
        for t in range(k * VIS_CHUNK, (k + 1) * VIS_CHUNK):
            patch, plane = patch_ref[t], plane_ref[t]
            slot = facet_ref[t] * NP + lax.rem(patch, 4) * 4 + lax.div(patch, 4)
            slot = jnp.where(t < count_ref[0], slot, SLOTS)
            real, imag = vis_buf[t, 0], vis_buf[t, 1]
            half = dot(lanes(real, imag), term_op[plane])
            half_real, half_imag = half[:, :S].astype(BF16), half[:, S:].astype(BF16)
            term = dot(
                back_op[plane], stack(lanes(half_real, half_imag), lanes(half_imag, -half_real))
            )
            acc[slot] += term
            cnt_acc[slot, pl.ds(plane, 1), :] += jnp.ones((1, S), F32)

    @pl.loop(0, SLOTS)
    def _(s):
        grid_ref[s] = acc[s].astype(BF16)
        cnt_ref[s] = cnt_acc[s].astype(BF16)


def regrid(w_kernels, visibilities, tile_facet, tile_patch, tile_wplane, tile_count):
    smem = pl.BlockSpec(memory_space=pltpu.SMEM)
    vmem = pl.BlockSpec(memory_space=pltpu.VMEM)
    return pl.pallas_call(
        regrid_kernel,
        out_shape=(
            jax.ShapeDtypeStruct((SLOTS, S, 2 * S), BF16),
            jax.ShapeDtypeStruct((SLOTS, WPLANES, S), BF16),
        ),
        in_specs=[smem] * 4 + [vmem, pl.BlockSpec(memory_space=pl.ANY)],
        out_specs=(vmem, vmem),
        scratch_shapes=[
            pltpu.VMEM((TILE_CAP, 2, S, S), BF16),
            pltpu.VMEM((WPLANES, S, 2 * S), BF16),
            pltpu.VMEM((WPLANES, 2 * S, 2 * S), BF16),
            pltpu.VMEM((SLOTS + 1, S, 2 * S), F32),
            pltpu.VMEM((SLOTS + 1, WPLANES, S), F32),
            pltpu.SemaphoreType.DMA((TILE_CAP // VIS_CHUNK,)),
        ],
        compiler_params=pltpu.CompilerParams(vmem_limit_bytes=40 << 20),
        name="regrid",
    )(tile_facet, tile_patch, tile_wplane, tile_count, w_kernels, visibilities)


def cycle_kernel(
    sky_ref, cs_ref, w_ref, cnt_ref, grid_hbm, out_ref,
    grid_buf, to_rows, to_cols, half_buf, column_buf, dirty_buf, dirty_in, u_buf, row_in,
    cnt_in, left_op, right_op, b_buf, wide_buf, grid_sems, send_sems, recv_sems, dirty_send, dirty_recv,
):
    me = lax.axis_index("vis")
    half_index = lax.rem(me, 2)
    column = lax.rem(lax.div(me, 2), 4)
    facet = lax.div(me, 8)

    grid_copies = [
        pltpu.make_async_copy(
            grid_hbm.at[pl.ds(f * NP, NP)], grid_buf.at[pl.ds(f * NP, NP)], grid_sems.at[f]
        )
        for f in range(F)
    ]
    for copy in grid_copies:
        copy.start()

    barrier = pltpu.get_barrier_semaphore()

    @pl.loop(1, DEVICES)
    def _(k):
        other = lax.rem(me + k, DEVICES)
        pl.semaphore_signal(barrier, inc=1, device_id={"vis": other}, device_id_type=MESH)

    for c in range(4):
        at, low = c * 2 * S, c * S
        to_cols[:, at:at + S] = cs_ref[0, :, low:low + S]
        to_cols[:, at + S:at + 2 * S] = -cs_ref[1, :, low:low + S]
        to_rows[at:at + S, :] = cs_ref[0, low:low + S, :]
        to_rows[at + S:at + 2 * S, :] = -cs_ref[1, low:low + S, :]

    def remote(src, dst, send, recv, other):
        return pltpu.make_async_remote_copy(
            src_ref=src, dst_ref=dst, send_sem=send, recv_sem=recv,
            device_id={"vis": other}, device_id_type=MESH,
        )

    def wait_for(ref, sem):
        pltpu.make_async_copy(ref, ref, sem).wait()

    def exchange_columns(stage):
        def piece(other):
            f, c = lax.div(other, 8), lax.rem(lax.div(other, 2), 4)
            return half_buf.at[
                stage,
                pl.ds(pl.multiple_of(f * ROWS, ROWS), ROWS),
                pl.ds(pl.multiple_of(c * 2 * S, 2 * S), 2 * S),
            ]

        def place():
            return column_buf.at[stage, me]

        @pl.loop(1, DEVICES)
        def _(k):
            other = lax.rem(me + k, DEVICES)
            remote(piece(other), place(), send_sems.at[2 * stage], recv_sems.at[2 * stage], other).start()

        pltpu.make_async_copy(piece(me), place(), recv_sems.at[2 * stage]).start()

    def exchange_rows(stage):
        def piece(other):
            return u_buf.at[stage, pl.ds(pl.multiple_of(other * ROWS, ROWS), ROWS), :]

        def place():
            block = column * 2 + half_index
            return row_in.at[stage, block, pl.ds(pl.multiple_of(facet * ROWS, ROWS), ROWS), :]

        @pl.loop(1, DEVICES)
        def _(k):
            other = lax.rem(me + k, DEVICES)
            remote(
                piece(other), place(), send_sems.at[2 * stage + 1], recv_sems.at[2 * stage + 1], other
            ).start()

        pltpu.make_async_copy(piece(me), place(), recv_sems.at[2 * stage + 1]).start()

    half_buf[0] = dot(sky_ref[0], to_cols[...]).astype(BF16)
    pl.semaphore_wait(barrier, DEVICES - 1)

    @pl.loop(1, DEVICES)
    def _(k):
        other = lax.rem(me + k, DEVICES)
        remote(cnt_ref.at[other], cnt_in.at[me], send_sems.at[4], recv_sems.at[4], other).start()

    pltpu.make_async_copy(cnt_ref.at[me], cnt_in.at[me], recv_sems.at[4]).start()
    exchange_columns(0)

    for f in range(F):
        grid_copies[f].wait()
        for c in range(4):
            at = f * NP + c * 4
            block = grid_buf[at:at + 4].reshape(P_SIZE, 2 * S)
            cosine_part, sine_part = dot(cs_ref[0], block), dot(cs_ref[1], block)
            wide_buf[:, c * 2 * S:c * 2 * S + S] = (cosine_part[:, :S] - sine_part[:, S:]).astype(BF16)
            wide_buf[:, c * 2 * S + S:(c + 1) * 2 * S] = (cosine_part[:, S:] + sine_part[:, :S]).astype(BF16)
        dirty_buf[f] = dot(wide_buf[...], to_rows[...]).astype(BF16)

        @pl.loop(1, DEVICES)
        def _(k):
            other = lax.rem(me + k, DEVICES)
            remote(
                dirty_buf.at[f, pl.ds(pl.multiple_of(other * ROWS, ROWS), ROWS), :],
                dirty_in.at[f, me], dirty_send.at[f], dirty_recv.at[f], other,
            ).start()

        pltpu.make_async_copy(
            dirty_buf.at[f, pl.ds(pl.multiple_of(me * ROWS, ROWS), ROWS), :],
            dirty_in.at[f, me], dirty_recv.at[f],
        ).start()

    @pl.loop(0, WPLANES)
    def _(w):
        real, imag = w_ref[w, 0], w_ref[w, 1]
        gram = dot(lanes(real.T, imag.T), stack(lanes(real, imag), lanes(imag, -real))).astype(BF16)
        gram_real, gram_imag = gram[:, :S], gram[:, S:]
        left_op[pl.ds(w * S, S), :] = gram
        right_op[pl.ds(w * 2 * S, S), :] = lanes(gram_real, -gram_imag)
        right_op[pl.ds(w * 2 * S + S, S), :] = lanes(gram_imag, gram_real)

    wait_for(cnt_in, recv_sems.at[4])
    counts = jnp.sum(cnt_in[...].astype(F32), axis=0)

    rows_at = pl.multiple_of(half_index * 2 * S, 2 * S)

    def model_rows(stage):
        wait_for(column_buf.at[stage], recv_sems.at[2 * stage])
        half = column_buf[stage].reshape(P_SIZE, 2 * S)
        turned = lanes(half[:, S:], -half[:, :S])
        grid = dot(cs_ref[0, pl.ds(rows_at, 2 * S), :], half) + dot(cs_ref[1, pl.ds(rows_at, 2 * S), :], turned)
        grid = grid.astype(BF16)
        for q in range(2):
            patch = grid[q * S:(q + 1) * S]
            operand = stack(patch, lanes(-patch[:, S:], patch[:, :S]))
            for w in range(WPLANES):
                part = dot(left_op[w * S:(w + 1) * S, :], operand)
                scale = counts[q, w:w + 1, :]
                b_buf[q * S:(q + 1) * S, w * 2 * S:(w + 1) * 2 * S] = (part * lanes(scale, scale)).astype(BF16)
        model = dot(b_buf[...], right_op[...]).astype(BF16)
        turned = lanes(-model[:, S:], model[:, :S])
        u_buf[stage] = (
            dot(cs_ref[0, :, pl.ds(rows_at, 2 * S)], model) + dot(cs_ref[1, :, pl.ds(rows_at, 2 * S)], turned)
        ).astype(BF16)
        exchange_rows(stage)
        wait_for(row_in.at[stage], recv_sems.at[2 * stage + 1])
        parts = [
            (row_in[stage, 2 * c].astype(F32) + row_in[stage, 2 * c + 1].astype(F32)).astype(BF16)
            for c in range(4)
        ]
        return dot(lanes(*parts), to_rows[...])

    image = model_rows(0)
    for f in range(F):
        wait_for(dirty_in.at[f], dirty_recv.at[f])
        dirty = jnp.sum(dirty_in[f].astype(F32), axis=0)
        out_ref[f * ROWS:(f + 1) * ROWS, :] = dirty
    residual = (out_ref[...] - image) * WEIGHT
    sky = (sky_ref[1].astype(F32) + LOOP_GAIN * residual).astype(BF16)
    half_buf[1] = dot(sky, to_cols[...]).astype(BF16)
    exchange_columns(1)
    image = model_rows(1)
    out_ref[...] = (out_ref[...] - image) * WEIGHT

    for stage in range(2):
        wait_for(column_buf.at[stage, pl.ds(0, DEVICES - 1)], send_sems.at[2 * stage])
        wait_for(u_buf.at[stage, pl.ds(0, P_SIZE - ROWS), :], send_sems.at[2 * stage + 1])
    wait_for(cnt_in.at[pl.ds(0, DEVICES - 1)], send_sems.at[4])
    for f in range(F):
        wait_for(dirty_in.at[f, pl.ds(0, DEVICES - 1)], dirty_send.at[f])


def cycles(sky, tables, w_kernels, counts, grid):
    vmem = pl.BlockSpec(memory_space=pltpu.VMEM)
    return pl.pallas_call(
        cycle_kernel,
        out_shape=jax.ShapeDtypeStruct((F * ROWS, P_SIZE), F32),
        in_specs=[vmem] * 4 + [pl.BlockSpec(memory_space=pl.ANY)],
        out_specs=vmem,
        scratch_shapes=[
            pltpu.VMEM((SLOTS, S, 2 * S), BF16),
            pltpu.VMEM((2 * P_SIZE, P_SIZE), BF16),
            pltpu.VMEM((P_SIZE, 2 * P_SIZE), BF16),
            pltpu.VMEM((2, F * ROWS, 2 * P_SIZE), BF16),
            pltpu.VMEM((2, DEVICES, ROWS, 2 * S), BF16),
            pltpu.VMEM((F, P_SIZE, P_SIZE), BF16),
            pltpu.VMEM((F, DEVICES, ROWS, P_SIZE), BF16),
            pltpu.VMEM((2, P_SIZE, 2 * S), BF16),
            pltpu.VMEM((2, 8, F * ROWS, 2 * S), BF16),
            pltpu.VMEM((DEVICES, 2, WPLANES, S), BF16),
            pltpu.VMEM((WPLANES * S, 2 * S), BF16),
            pltpu.VMEM((WPLANES * 2 * S, 2 * S), BF16),
            pltpu.VMEM((2 * S, WPLANES * 2 * S), BF16),
            pltpu.VMEM((P_SIZE, 2 * P_SIZE), BF16),
            pltpu.SemaphoreType.DMA((F,)),
            pltpu.SemaphoreType.DMA((5,)),
            pltpu.SemaphoreType.DMA((5,)),
            pltpu.SemaphoreType.DMA((F,)),
            pltpu.SemaphoreType.DMA((F,)),
        ],
        compiler_params=pltpu.CompilerParams(
            collective_id=0, has_side_effects=True, vmem_limit_bytes=48 << 20
        ),
        name="cycles",
    )(sky, tables, w_kernels, counts, grid)


def dft_tables():
    phases = np.outer(np.arange(P_SIZE), np.arange(P_SIZE)) % P_SIZE
    angles = phases * (2.0 * math.pi / P_SIZE)
    return (np.stack([np.cos(angles), np.sin(angles)]) / math.sqrt(P_SIZE)).astype(BF16)


def local(model_input, w_kernels, visibilities, tile_facet, tile_patch, tile_wplane, tile_count):
    grid, counts = regrid(w_kernels, visibilities, tile_facet, tile_patch, tile_wplane, tile_count)
    sky = model_input.reshape(2, F * ROWS, P_SIZE)
    counts = counts.reshape(DEVICES, 2, WPLANES, S)
    image = cycles(sky, jnp.asarray(dft_tables()), w_kernels, counts, grid)
    return image.reshape(F, ROWS, P_SIZE)


def solution(mesh):
    return jax.shard_map(
        local,
        mesh=mesh,
        in_specs=(
            P(None, "freq", "vis", None),
            P("freq", None, None, None),
            P(("freq", "vis"), None, None, None),
            P(("freq", "vis")),
            P(("freq", "vis")),
            P(("freq", "vis")),
            P(("freq", "vis")),
        ),
        out_specs=P("freq", "vis", None),
        check_vma=False,
    )
```

time: 1290 us -> 74.9 us (0.06)
  waiting for transfers between devices: 950 us -> 0 us
  matrix products: 114 us -> 0 us
  local copies, waits for them, and re-layouts: 116 us -> 10.7 us
  Pallas kernels: 0 us -> 63.2 us
  other arithmetic: 52.7 us -> 0 us
  blocking collectives: 33.1 us -> 0 us
  between operations: 14.4 us -> 0.69 us
    psum x2 -> x0, waiting for transfers between devices: 643 us -> none  [local(): lax.psum(resid_grid.astype(jnp.bfloat16), 'vis').astype(jnp.float32)]
    all_gather x2 -> x0, waiting for transfers between devices: 307 us -> none  [local(): full_grid = lax.all_gather(grid_part, 'vis', axis=3, tiled=True)]
    dot_general x96 -> x0, matrix products: 114 us -> none  [the longest x76 74.3 us: lowprec(): jnp.einsum(pattern, first_op, second_op, preferred_element_type=jnp.float32)]
    pallas_call x0 -> x2, Pallas kernels: none -> 63.2 us  [the longest x1 56.3 us: cycles(): pl.pallas_call(cycle_kernel, out_shape=jax.ShapeDtypeStruct((F * ROWS, P_...]
    scatter-add x4 -> x0, other arithmetic: 42.3 us -> none  [accumulate(): return (running.at[slot_ids].add(tile_sums), None)]
    convert_element_type x6 -> x0, local copies, waits for them, and re-layouts: 35.1 us -> none  [local(): resid_grid.astype(jnp.bfloat16)]
    all_to_all x2 -> x0, blocking collectives: 33.1 us -> none  [local(): lax.all_to_all(half_grid, 'vis', split_axis=3, concat_axis=2, tiled=True)]
    reshape x6 -> x0, local copies, waits for them, and re-layouts: 28.8 us -> none  [the longest x2 14.6 us: local(): patch_table = full_grid.reshape(F, 2, P_SIZE // S, S, P_SIZE // S, S).tra...]
  transfers between devices with their start and end apart: 4 -> 0, of which waited for: 4 -> 0; matrix products, arithmetic and copies ran while one was open for 0% -> 0% of each run, Pallas kernels for 0% -> 0%
where the time goes in v1:
time: 74.9 us; the launch traced here: 74.6 us
  Pallas kernels  63.2 us (84%)
  local copies, waits for them, and re-layouts  10.7 us (14%)
    pallas_call x1, Pallas kernels, cycles(): pl.pallas_call(cycle_kernel, out_shape=jax.ShapeDtypeStruct((F * ROWS, P_...  56.3 us
    unnamed x19, local copies, waits for them, and re-layouts  10.7 us
    pallas_call x1, Pallas kernels, regrid(): pl.pallas_call(regrid_kernel, out_shape=(jax.ShapeDtypeStruct((SLOTS, S,...  6.93 us

profile of v1, /device:TPU:0, one launch (start us, length us, event | category | flops | bytes accessed | tf_op | source)
XLA Modules:
  0.0 74.6 jit_solution(3119713068553445910)
XLA Ops:
  0.7 0.0 copy-start.1
  0.7 1.2 %copy-done.1 = bf16[16,2,128,128]{3,2,1,0:T(8,128)(2,1)S(1)} copy-done((bf16[16,2,128,128]{3,2,1,0:T(8,128)(2,1)S(1)}, bf16[16,2,128,128]{3,2,1,0:T(8,128)(2,1)}, u32[]{:S(2)}) %copy-start.1) | copy-done | bytes 1048600
  1.9 0.0 copy-start.3
  1.9 1.6 %copy-done.3 = bf16[32,2,128,128]{3,2,1,0:T(8,128)(2,1)S(1)} copy-done((bf16[32,2,128,128]{3,2,1,0:T(8,128)(2,1)S(1)}, bf16[32,2,128,128]{3,2,1,0:T(8,128)(2,1)}, u32[]{:S(2)}) %copy-start.3) | copy-done | bytes 2097176
  3.5 0.0 copy-start.6
  3.5 0.7 copy-done.6
  4.1 0.0 copy-start.7
  4.1 0.7 copy-done.7
  4.8 0.0 copy-start.8
  4.8 0.7 copy-done.8
  5.4 6.9 %regrid.1 = (bf16[64,128,256]{2,1,0:T(8,128)(2,1)S(1)}, bf16[64,16,128]{2,1,0:T(8,128)(2,1)S(1)}) custom-call(s32[32]{0:T(128)S(1)} %copy-done.6, s32[32]{0:T(128)S(1)} %copy-done.7, s32[32]{0:T(128)S(1)} %copy-done.8, s32[1]{0:T(128)S(6)} %copy.10.count_ref, bf16[16,2,128,128]{3,2,1,0:T(8,128)(2,1)S(1)} %copy-done.1, bf16[32,2,128,128]{3,2,1,0:T(8,128)(2,1)S(1)} %copy-done.3), custom_call_target="tpu_custom_call" | custom-call | tf_op jit(solution)/shard_map/regrid/pallas_call | solution.py:92
  12.4 0.0 copy-start
  12.4 1.9 %copy-done = bf16[64,128,256]{2,1,0:T(8,128)(2,1)} copy-done((bf16[64,128,256]{2,1,0:T(8,128)(2,1)}, bf16[64,128,256]{2,1,0:T(8,128)(2,1)S(1)}, u32[]{:S(2)}) %copy-start) | copy-done | bytes 4194328
  14.3 0.0 copy-start.2
  14.3 1.2 %copy-done.2 = bf16[16,2,128,128]{3,2,1,0:T(8,128)(2,1)S(1)} copy-done((bf16[16,2,128,128]{3,2,1,0:T(8,128)(2,1)S(1)}, bf16[16,2,128,128]{3,2,1,0:T(8,128)(2,1)}, u32[]{:S(2)}) %copy-start.2) | copy-done | bytes 1048600
  15.5 0.0 copy-start.4
  15.6 1.2 %copy-done.4 = bf16[2,512,512]{2,1,0:T(8,128)(2,1)S(1)} copy-done((bf16[2,512,512]{2,1,0:T(8,128)(2,1)S(1)}, bf16[2,512,512]{2,1,0:T(8,128)(2,1)}, u32[]{:S(2)}) %copy-start.4) | copy-done | bytes 1048600
  16.8 0.0 copy-start.5
  16.8 0.9 %copy-done.5 = bf16[2,4,16,512]{3,2,1,0:T(8,128)(2,1)S(1)} copy-done((bf16[2,4,16,512]{3,2,1,0:T(8,128)(2,1)S(1)}, bf16[2,4,16,512]{3,2,1,0:T(8,128)(2,1)}, u32[]{:S(2)}) %copy-start.5) | copy-done | bytes 131096
  17.7 56.3 %cycles.1 = f32[64,512]{1,0:T(8,128)S(1)} custom-call(bf16[2,64,512]{2,1,0:T(8,128)(2,1)S(1)} %bitcast.5, bf16[2,512,512]{2,1,0:T(8,128)(2,1)S(1)} %copy-done.4, bf16[16,2,128,128]{3,2,1,0:T(8,128)(2,1)S(1)} %copy-done.2, bf16[32,2,16,128]{3,2,1,0:T(8,128)(2,1)S(1)} %bitcast.4, bf16[64,128,256]{2,1,0:T(8,128)(2,1)} %copy-done), custom_call_target="tpu_custom_call" | custom-call | tf_op jit(solution)/shard_map/cycles/pallas_call | solution.py:287
  74.0 0.7 copy.11
Async XLA Ops:
  0.7 1.2 %copy-start.1 = (bf16[16,2,128,128]{3,2,1,0:T(8,128)(2,1)S(1)}, bf16[16,2,128,128]{3,2,1,0:T(8,128)(2,1)}, u32[]{:S(2)}) copy-start(bf16[16,2,128,128]{3,2,1,0:T(8,128)(2,1)} %w_ref.3) | copy-start | bytes 3145732
  1.9 1.6 %copy-start.3 = (bf16[32,2,128,128]{3,2,1,0:T(8,128)(2,1)S(1)}, bf16[32,2,128,128]{3,2,1,0:T(8,128)(2,1)}, u32[]{:S(2)}) copy-start(bf16[32,2,128,128]{3,2,1,0:T(8,128)(2,1)} %vis_hbm.1) | copy-start | bytes 6291460
  3.5 0.7 copy-start.6
  4.1 0.7 copy-start.7
  4.8 0.7 copy-start.8
  12.4 1.9 %copy-start = (bf16[64,128,256]{2,1,0:T(8,128)(2,1)}, bf16[64,128,256]{2,1,0:T(8,128)(2,1)S(1)}, u32[]{:S(2)}) copy-start(bf16[64,128,256]{2,1,0:T(8,128)(2,1)S(1)} %get-tuple-element.8.grid_hbm) | copy-start | bytes 12582916
  14.3 1.2 %copy-start.2 = (bf16[16,2,128,128]{3,2,1,0:T(8,128)(2,1)S(1)}, bf16[16,2,128,128]{3,2,1,0:T(8,128)(2,1)}, u32[]{:S(2)}) copy-start(bf16[16,2,128,128]{3,2,1,0:T(8,128)(2,1)} %w_ref.3) | copy-start | bytes 3145732
  15.5 1.2 %copy-start.4 = (bf16[2,512,512]{2,1,0:T(8,128)(2,1)S(1)}, bf16[2,512,512]{2,1,0:T(8,128)(2,1)}, u32[]{:S(2)}) copy-start(bf16[2,512,512]{2,1,0:T(8,128)(2,1)} %constant.2.clone.cs_ref) | copy-start | bytes 3145732
  16.8 0.9 %copy-start.5 = (bf16[2,4,16,512]{3,2,1,0:T(8,128)(2,1)S(1)}, bf16[2,4,16,512]{3,2,1,0:T(8,128)(2,1)}, u32[]{:S(2)}) copy-start(bf16[2,4,16,512]{3,2,1,0:T(8,128)(2,1)} %param.8) | copy-start | bytes 393220

commit v2 on v1

v2 whole, which is shorter than its diff:
```python
import math

import jax
import jax.numpy as jnp
import numpy as np
from jax import lax
from jax.experimental import pallas as pl
from jax.experimental.pallas import tpu as pltpu
from jax.sharding import PartitionSpec as P

P_SIZE = 512
S = 128
F = 4
WPLANES = 16
TILE_CAP = 32
NP = 16
SLOTS = F * NP
DEVICES = 32
ROWS = P_SIZE // DEVICES
TILES = TILE_CAP * DEVICES
WEIGHT = math.sqrt(F * NP / TILES)
LOOP_GAIN = 0.5
MESH = pl.DeviceIdType.MESH
BF16 = jnp.bfloat16
F32 = jnp.float32
VIS_CHUNK = 4
CHUNKS = TILE_CAP // VIS_CHUNK


def dot(a, b):
    return lax.dot_general(a, b, (((1,), (0,)), ((), ())), preferred_element_type=F32)


def lanes(*parts):
    return jnp.concatenate(parts, axis=1)


def stack(*parts):
    return jnp.concatenate(parts, axis=0)


def imaging_kernel(
    facet_hbm, patch_hbm, plane_hbm, count_hbm, sky_hbm, cs_hbm, w_hbm, vis_hbm, out_ref,
    facet_ref, patch_ref, plane_ref, count_ref, sky_ref, cs_ref, w_ref, vis_buf,
    back_op, term_op, run_buf, grid_buf, to_rows, to_cols, half_buf, column_buf, u_buf, row_in,
    cnt_out, cnt_in, left_op, right_op, b_buf, wide_buf, model_buf,
    dirty_out, dirty_in, second_out, second_in, third_own, third_out, third_in,
    load_sems, vis_sems, send_sems, recv_sems, dirty_send, dirty_recv,
):
    me = lax.axis_index("vis")
    half_index = lax.rem(me, 2)
    column = lax.rem(lax.div(me, 2), 4)
    facet = lax.div(me, 8)
    at_x, at_y, at_z = lax.rem(me, 4), lax.rem(lax.div(me, 4), 4), lax.div(me, 16)

    loads = [
        pltpu.make_async_copy(src, dst, load_sems.at[k])
        for k, (src, dst) in enumerate(
            (
                (facet_hbm, facet_ref), (patch_hbm, patch_ref), (plane_hbm, plane_ref), (count_hbm, count_ref),
                (w_hbm, w_ref), (cs_hbm, cs_ref), (sky_hbm, sky_ref),
            )
        )
    ]
    vis_loads = [
        pltpu.make_async_copy(
            vis_hbm.at[pl.ds(k * VIS_CHUNK, VIS_CHUNK)],
            vis_buf.at[pl.ds(k * VIS_CHUNK, VIS_CHUNK)],
            vis_sems.at[k],
        )
        for k in range(CHUNKS)
    ]
    for copy in loads[:5] + vis_loads + loads[5:]:
        copy.start()

    barrier = pltpu.get_barrier_semaphore()

    @pl.loop(1, DEVICES)
    def _(k):
        other = lax.rem(me + k, DEVICES)
        pl.semaphore_signal(barrier, inc=1, device_id={"vis": other}, device_id_type=MESH)

    def remote(src, dst, send, recv, other):
        return pltpu.make_async_remote_copy(
            src_ref=src, dst_ref=dst, send_sem=send, recv_sem=recv,
            device_id={"vis": other}, device_id_type=MESH,
        )

    def wait_for(ref, sem):
        pltpu.make_async_copy(ref, ref, sem).wait()

    def to_all(piece, place, index):
        @pl.loop(1, DEVICES)
        def _(k):
            other = lax.rem(me + k, DEVICES)
            remote(piece(other), place, send_sems.at[index], recv_sems.at[index], other).start()

        pltpu.make_async_copy(piece(me), place, recv_sems.at[index]).start()

    def exchange_columns(stage):
        def piece(other):
            f, c = lax.div(other, 8), lax.rem(lax.div(other, 2), 4)
            return half_buf.at[
                stage,
                pl.ds(pl.multiple_of(f * ROWS, ROWS), ROWS),
                pl.ds(pl.multiple_of(c * 2 * S, 2 * S), 2 * S),
            ]

        to_all(piece, column_buf.at[stage, me], 2 * stage)

    def exchange_rows(stage):
        def piece(other):
            return u_buf.at[stage, pl.ds(pl.multiple_of(other * ROWS, ROWS), ROWS), :]

        place = row_in.at[
            stage, column * 2 + half_index, pl.ds(pl.multiple_of(facet * ROWS, ROWS), ROWS), :
        ]
        to_all(piece, place, 2 * stage + 1)

    for copy in loads[:4]:
        copy.wait()

    lane = lax.broadcasted_iota(jnp.int32, (1, S), 1)
    tile = lax.broadcasted_iota(jnp.int32, (TILE_CAP, S), 0)
    slot_row = jnp.full((1, S), SLOTS, jnp.int32)
    plane_row = jnp.full((1, S), WPLANES, jnp.int32)
    slot_column = jnp.full((TILE_CAP, S), SLOTS, jnp.int32)
    for t in range(TILE_CAP):
        patch = patch_ref[t]
        slot = facet_ref[t] * NP + lax.rem(patch, 4) * 4 + lax.div(patch, 4)
        slot = jnp.where(t < count_ref[0], slot, SLOTS)
        slot_row = jnp.where(lane == t, slot, slot_row)
        plane_row = jnp.where(lane == t, plane_ref[t], plane_row)
        slot_column = jnp.where(tile == t, slot, slot_column)
    tile_lane = lax.broadcasted_iota(jnp.int32, (TILE_CAP, S), 1)
    before = jnp.max(
        jnp.where((slot_column == slot_row) & (tile_lane < tile), tile_lane, -1), axis=1, keepdims=True
    )
    slot_lane = lax.broadcasted_iota(jnp.int32, (SLOTS, S), 1)
    member = lax.broadcasted_iota(jnp.int32, (SLOTS, S), 0) == slot_row
    last = jnp.max(jnp.where(member, slot_lane, -1), axis=1, keepdims=True)
    before = jnp.where(before < 0, TILE_CAP, before)
    last = jnp.where(last < 0, TILE_CAP, last)

    in_plane = jnp.where(
        lax.broadcasted_iota(jnp.int32, (WPLANES, S), 0) == plane_row, 1.0, 0.0
    )
    in_slot = jnp.where(member, 1.0, 0.0)
    pairs = stack(*[(in_plane * in_slot[s:s + 1, :]).astype(BF16) for s in range(SLOTS)])
    cnt_out[...] = dot(pairs, jnp.ones((S, S), BF16)).astype(BF16).reshape(DEVICES, 2, WPLANES, S)

    loads[4].wait()

    @pl.loop(0, WPLANES)
    def _(w):
        real, imag = w_ref[w, 0], w_ref[w, 1]
        back_op[w] = lanes(real.T, imag.T)
        term_op[w] = stack(lanes(real, -imag), lanes(imag, real))

    run_buf[TILE_CAP] = jnp.zeros((S, 2 * S), F32)
    for k in range(CHUNKS):
        vis_loads[k].wait()
        for t in range(k * VIS_CHUNK, (k + 1) * VIS_CHUNK):
            plane = plane_ref[t]
            real, imag = vis_buf[t, 0], vis_buf[t, 1]
            half = dot(lanes(real, imag), term_op[plane])
            half_real, half_imag = half[:, :S].astype(BF16), half[:, S:].astype(BF16)
            term = dot(
                back_op[plane], stack(lanes(half_real, half_imag), lanes(half_imag, -half_real))
            )
            run_buf[t] = term + run_buf[before[t, 0]]

    loads[5].wait()
    for c in range(4):
        at, low = c * 2 * S, c * S
        to_cols[:, at:at + S] = cs_ref[0, :, low:low + S]
        to_cols[:, at + S:at + 2 * S] = -cs_ref[1, :, low:low + S]
        to_rows[at:at + S, :] = cs_ref[0, low:low + S, :]
        to_rows[at + S:at + 2 * S, :] = -cs_ref[1, low:low + S, :]
    loads[6].wait()
    half_buf[0] = dot(sky_ref[0], to_cols[...]).astype(BF16)
    pl.semaphore_wait(barrier, DEVICES - 1)
    to_all(lambda other: cnt_out.at[other], cnt_in.at[me], 4)
    exchange_columns(0)

    def first_stage(f):
        for k in range(1, 4):
            if f % 2 == 0:
                x = lax.rem(at_x + k, 4)
                piece, other = dirty_out.at[f, :, :, x], at_z * 16 + at_y * 4 + x
            else:
                y = lax.rem(at_y + k, 4)
                piece, other = dirty_out.at[f, :, y], at_z * 16 + y * 4 + at_x
            remote(piece, dirty_in.at[f, k - 1], dirty_send.at[0, f], dirty_recv.at[0, f], other).start()

    def second_stage(f):
        wait_for(dirty_in.at[f], dirty_recv.at[0, f])
        mine = dirty_out[f, :, :, at_x] if f % 2 == 0 else dirty_out[f, :, at_y]
        total = mine.astype(F32)
        for k in range(3):
            total += dirty_in[f, k].astype(F32)
        second_out[f] = total.astype(BF16)
        for k in range(1, 4):
            if f % 2 == 0:
                step = lax.rem(at_y + k, 4)
                other = at_z * 16 + step * 4 + at_x
            else:
                step = lax.rem(at_x + k, 4)
                other = at_z * 16 + at_y * 4 + step
            remote(
                second_out.at[f, :, step], second_in.at[f, k - 1], dirty_send.at[1, f], dirty_recv.at[1, f], other
            ).start()

    def third_stage(f):
        wait_for(second_in.at[f], dirty_recv.at[1, f])
        total = second_out[f, :, at_y if f % 2 == 0 else at_x].astype(F32)
        for k in range(3):
            total += second_in[f, k].astype(F32)
        third_own[f] = total
        third_out[f] = total.astype(BF16)
        remote(
            third_out.at[f, 1 - at_z], third_in.at[f], dirty_send.at[2, f], dirty_recv.at[2, f],
            lax.rem(me + 16, DEVICES),
        ).start()

    def dirty_rows(f):
        wait_for(third_in.at[f], dirty_recv.at[2, f])
        return third_own[f, at_z] + third_in[f].astype(F32)

    for f in range(F):
        for s in range(NP):
            grid_buf[s] = run_buf[last[f * NP + s, 0]].astype(BF16)
        for c in range(4):
            block = grid_buf[c * 4:c * 4 + 4].reshape(P_SIZE, 2 * S)
            cosine_part, sine_part = dot(cs_ref[0], block), dot(cs_ref[1], block)
            wide_buf[:, c * 2 * S:c * 2 * S + S] = (cosine_part[:, :S] - sine_part[:, S:]).astype(BF16)
            wide_buf[:, c * 2 * S + S:(c + 1) * 2 * S] = (cosine_part[:, S:] + sine_part[:, :S]).astype(BF16)
        dirty_out[f] = dot(wide_buf[...], to_rows[...]).astype(BF16).reshape(2, 4, 4, ROWS, P_SIZE)
        first_stage(f)

    @pl.loop(0, WPLANES)
    def _(w):
        real, imag = w_ref[w, 0], w_ref[w, 1]
        gram = dot(back_op[w], stack(lanes(real, imag), lanes(imag, -real))).astype(BF16)
        gram_real, gram_imag = gram[:, :S], gram[:, S:]
        left_op[pl.ds(w * S, S), :] = gram
        right_op[pl.ds(w * 2 * S, S), :] = lanes(gram_real, -gram_imag)
        right_op[pl.ds(w * 2 * S + S, S), :] = lanes(gram_imag, gram_real)

    wait_for(cnt_in, recv_sems.at[4])
    counts = jnp.sum(cnt_in[...].astype(F32), axis=0)

    rows_at = pl.multiple_of(half_index * 2 * S, 2 * S)

    def model_slots(stage):
        wait_for(column_buf.at[stage], recv_sems.at[2 * stage])
        half = column_buf[stage].reshape(P_SIZE, 2 * S)
        turned = lanes(half[:, S:], -half[:, :S])
        grid = dot(cs_ref[0, pl.ds(rows_at, 2 * S), :], half) + dot(cs_ref[1, pl.ds(rows_at, 2 * S), :], turned)
        grid = grid.astype(BF16)
        for q in range(2):
            patch = grid[q * S:(q + 1) * S]
            operand = stack(patch, lanes(-patch[:, S:], patch[:, :S]))
            for w in range(WPLANES):
                part = dot(left_op[w * S:(w + 1) * S, :], operand)
                scale = counts[q, w:w + 1, :]
                b_buf[q * S:(q + 1) * S, w * 2 * S:(w + 1) * 2 * S] = (part * lanes(scale, scale)).astype(BF16)
        model = dot(b_buf[...], right_op[...]).astype(BF16)
        turned = lanes(-model[:, S:], model[:, :S])
        u_buf[stage] = (
            dot(cs_ref[0, :, pl.ds(rows_at, 2 * S)], model) + dot(cs_ref[1, :, pl.ds(rows_at, 2 * S)], turned)
        ).astype(BF16)
        exchange_rows(stage)

    def model_rows(stage):
        wait_for(row_in.at[stage], recv_sems.at[2 * stage + 1])
        parts = [
            (row_in[stage, 2 * c].astype(F32) + row_in[stage, 2 * c + 1].astype(F32)).astype(BF16)
            for c in range(4)
        ]
        return dot(lanes(*parts), to_rows[...])

    model_slots(0)
    second_stage(0)
    second_stage(1)
    model_buf[...] = model_rows(0)
    third_stage(0)
    third_stage(1)
    second_stage(2)
    second_stage(3)
    third_stage(2)
    third_stage(3)
    for f in range(F):
        out_ref[f * ROWS:(f + 1) * ROWS, :] = dirty_rows(f)
    residual = (out_ref[...] - model_buf[...]) * WEIGHT
    sky = (sky_ref[1].astype(F32) + LOOP_GAIN * residual).astype(BF16)
    half_buf[1] = dot(sky, to_cols[...]).astype(BF16)
    exchange_columns(1)
    model_slots(1)
    out_ref[...] = (out_ref[...] - model_rows(1)) * WEIGHT

    for stage in range(2):
        wait_for(column_buf.at[stage, pl.ds(0, DEVICES - 1)], send_sems.at[2 * stage])
        wait_for(u_buf.at[stage, pl.ds(0, P_SIZE - ROWS), :], send_sems.at[2 * stage + 1])
    wait_for(cnt_in.at[pl.ds(0, DEVICES - 1)], send_sems.at[4])
    for f in range(F):
        wait_for(dirty_in.at[f], dirty_send.at[0, f])
        wait_for(second_in.at[f], dirty_send.at[1, f])
        wait_for(third_in.at[f], dirty_send.at[2, f])


def imaging(*operands):
    hbm = pl.BlockSpec(memory_space=pltpu.HBM)
    return pl.pallas_call(
        imaging_kernel,
        out_shape=jax.ShapeDtypeStruct((F * ROWS, P_SIZE), F32),
        in_specs=[hbm] * 8,
        out_specs=pl.BlockSpec(memory_space=pltpu.VMEM),
        scratch_shapes=[
            pltpu.SMEM((TILE_CAP,), jnp.int32),
            pltpu.SMEM((TILE_CAP,), jnp.int32),
            pltpu.SMEM((TILE_CAP,), jnp.int32),
            pltpu.SMEM((1,), jnp.int32),
            pltpu.VMEM((2, F * ROWS, P_SIZE), BF16),
            pltpu.VMEM((2, P_SIZE, P_SIZE), BF16),
            pltpu.VMEM((WPLANES, 2, S, S), BF16),
            pltpu.VMEM((TILE_CAP, 2, S, S), BF16),
            pltpu.VMEM((WPLANES, S, 2 * S), BF16),
            pltpu.VMEM((WPLANES, 2 * S, 2 * S), BF16),
            pltpu.VMEM((TILE_CAP + 1, S, 2 * S), F32),
            pltpu.VMEM((NP, S, 2 * S), BF16),
            pltpu.VMEM((2 * P_SIZE, P_SIZE), BF16),
            pltpu.VMEM((P_SIZE, 2 * P_SIZE), BF16),
            pltpu.VMEM((2, F * ROWS, 2 * P_SIZE), BF16),
            pltpu.VMEM((2, DEVICES, ROWS, 2 * S), BF16),
            pltpu.VMEM((2, P_SIZE, 2 * S), BF16),
            pltpu.VMEM((2, 8, F * ROWS, 2 * S), BF16),
            pltpu.VMEM((DEVICES, 2, WPLANES, S), BF16),
            pltpu.VMEM((DEVICES, 2, WPLANES, S), BF16),
            pltpu.VMEM((WPLANES * S, 2 * S), BF16),
            pltpu.VMEM((WPLANES * 2 * S, 2 * S), BF16),
            pltpu.VMEM((2 * S, WPLANES * 2 * S), BF16),
            pltpu.VMEM((P_SIZE, 2 * P_SIZE), BF16),
            pltpu.VMEM((F * ROWS, P_SIZE), F32),
            pltpu.VMEM((F, 2, 4, 4, ROWS, P_SIZE), BF16),
            pltpu.VMEM((F, 3, 2, 4, ROWS, P_SIZE), BF16),
            pltpu.VMEM((F, 2, 4, ROWS, P_SIZE), BF16),
            pltpu.VMEM((F, 3, 2, ROWS, P_SIZE), BF16),
            pltpu.VMEM((F, 2, ROWS, P_SIZE), F32),
            pltpu.VMEM((F, 2, ROWS, P_SIZE), BF16),
            pltpu.VMEM((F, ROWS, P_SIZE), BF16),
            pltpu.SemaphoreType.DMA((7,)),
            pltpu.SemaphoreType.DMA((CHUNKS,)),
            pltpu.SemaphoreType.DMA((5,)),
            pltpu.SemaphoreType.DMA((5,)),
            pltpu.SemaphoreType.DMA((3, F)),
            pltpu.SemaphoreType.DMA((3, F)),
        ],
        compiler_params=pltpu.CompilerParams(
            collective_id=0, has_side_effects=True, vmem_limit_bytes=56 << 20
        ),
        name="imaging",
    )(*operands)


def dft_tables():
    phases = np.outer(np.arange(P_SIZE), np.arange(P_SIZE)) % P_SIZE
    angles = phases * (2.0 * math.pi / P_SIZE)
    return (np.stack([np.cos(angles), np.sin(angles)]) / math.sqrt(P_SIZE)).astype(BF16)


def local(model_input, w_kernels, visibilities, tile_facet, tile_patch, tile_wplane, tile_count):
    sky = model_input.reshape(2, F * ROWS, P_SIZE)
    image = imaging(
        tile_facet, tile_patch, tile_wplane, tile_count,
        sky, jnp.asarray(dft_tables()), w_kernels, visibilities,
    )
    return image.reshape(F, ROWS, P_SIZE)


def solution(mesh):
    return jax.shard_map(
        local,
        mesh=mesh,
        in_specs=(
            P(None, "freq", "vis", None),
            P("freq", None, None, None),
            P(("freq", "vis"), None, None, None),
            P(("freq", "vis")),
            P(("freq", "vis")),
            P(("freq", "vis")),
            P(("freq", "vis")),
        ),
        out_specs=P("freq", "vis", None),
        check_vma=False,
    )
```

time: 74.9 us -> 61.3 us (0.82)
  local copies, waits for them, and re-layouts: 10.7 us -> 1.57 us
  Pallas kernels: 63.2 us -> 58.9 us
    unnamed x19 -> x1, local copies, waits for them, and re-layouts: 10.7 us -> 1.57 us
    pallas_call x2 -> x1, Pallas kernels: 63.2 us -> 58.9 us  [imaging(): pl.pallas_call(imaging_kernel, out_shape=jax.ShapeDtypeStruct((F * ROWS,...]
where the time goes in v2:
time: 61.3 us; the launch traced here: 61.1 us
  Pallas kernels  58.9 us (96%)
  local copies, waits for them, and re-layouts  1.57 us (3%)
  between operations  0.66 us (1%)
    pallas_call x1, Pallas kernels, imaging(): pl.pallas_call(imaging_kernel, out_shape=jax.ShapeDtypeStruct((F * ROWS,...  58.9 us
    unnamed x1, local copies, waits for them, and re-layouts  1.57 us

profile of v2, /device:TPU:0, one launch (start us, length us, event | category | flops | bytes accessed | tf_op | source)
XLA Modules:
  0.0 61.1 jit_solution(5633094263175124619)
XLA Ops:
  0.7 58.9 %imaging.1 = f32[64,512]{1,0:T(8,128)} custom-call(s32[32]{0:T(128)} %facet_hbm.1, s32[32]{0:T(128)} %patch_hbm.1, s32[32]{0:T(128)} %plane_hbm.1, s32[1]{0:T(128)S(6)} %copy.10.count_hbm, bf16[2,64,512]{2,1,0:T(8,128)(2,1)} %bitcast.3, bf16[2,512,512]{2,1,0:T(8,128)(2,1)} %constant.2.clone.cs_hbm, bf16[16,2,128,128]{3,2,1,0:T(8,128)(2,1)} %w_hbm.1, ...), custom_call_target="tpu_custom_call" | custom-call | tf_op jit(solution)/shard_map/imaging/pallas_call | solution.py:314
  59.6 1.6 %copy.11 = f32[4,16,512]{2,1,0:T(8,128)} copy(f32[4,16,512]{2,1,0:T(8,128)} %bitcast.2) | data formatting | bytes 262144

commit v3 on v2

v3 whole, which is shorter than its diff:
```python
import math

import jax
import jax.numpy as jnp
import numpy as np
from jax import lax
from jax.experimental import pallas as pl
from jax.experimental.pallas import tpu as pltpu
from jax.sharding import PartitionSpec as P

P_SIZE = 512
S = 128
F = 4
WPLANES = 16
TILE_CAP = 32
NP = 16
SLOTS = F * NP
DEVICES = 32
ROWS = P_SIZE // DEVICES
TILES = TILE_CAP * DEVICES
WEIGHT = math.sqrt(F * NP / TILES)
LOOP_GAIN = 0.5
MESH = pl.DeviceIdType.MESH
BF16 = jnp.bfloat16
F32 = jnp.float32
VIS_CHUNK = 4
CHUNKS = TILE_CAP // VIS_CHUNK
EXT = S + ROWS
WIDE = 3 * S


def dot(a, b):
    return lax.dot_general(a, b, (((1,), (0,)), ((), ())), preferred_element_type=F32)


def lanes(*parts):
    return jnp.concatenate(parts, axis=1)


def stack(*parts):
    return jnp.concatenate(parts, axis=0)


def owner(device):
    z, y, x = lax.div(device, 16), lax.rem(lax.div(device, 4), 4), lax.rem(device, 4)
    a, b = y + z * (x - y), x + z * (y - x)
    return 2 * z + lax.div(a, 2), lax.rem(a, 2), b


def static_owner(device):
    z, y, x = device // 16, device // 4 % 4, device % 4
    a, b = (x, y) if z else (y, x)
    return 2 * z + a // 2, a % 2, b


def slot_of(f, row, column):
    return f * NP + column * 4 + row


def where_equal(shape, rule):
    row = lax.broadcasted_iota(jnp.int32, shape, 0)
    column = lax.broadcasted_iota(jnp.int32, shape, 1)
    return rule(row, column).astype(BF16)


def one_if(condition):
    return jnp.where(condition, 1.0, 0.0)


def imaging_kernel(
    facet_hbm, patch_hbm, plane_hbm, count_hbm, sky_hbm, cs_hbm, edge_hbm, w_hbm, vis_hbm, out_ref,
    facet_ref, patch_ref, plane_ref, count_ref, sky_ref, cs_ref, edge_ref, w_ref, vis_buf,
    back_op, term_op, run_buf, grid_buf, to_rows, to_cols, half_buf, column_buf, u_buf, row_in,
    cnt_out, cnt_in, left_op, right_op, b_buf, spread_buf,
    first_out, first_in, second_out, second_in, third_own, third_out, third_in,
    load_sems, vis_sems, send_sems, recv_sems, dirty_send, dirty_recv,
):
    me = lax.axis_index("vis")
    facet, row_block, column = owner(me)
    at_x, at_y, at_z = lax.rem(me, 4), lax.rem(lax.div(me, 4), 4), lax.div(me, 16)

    loads = [
        pltpu.make_async_copy(src, dst, load_sems.at[k])
        for k, (src, dst) in enumerate(
            (
                (facet_hbm, facet_ref), (patch_hbm, patch_ref), (plane_hbm, plane_ref), (count_hbm, count_ref),
                (w_hbm, w_ref), (cs_hbm, cs_ref), (sky_hbm, sky_ref), (edge_hbm, edge_ref),
            )
        )
    ]
    vis_loads = [
        pltpu.make_async_copy(
            vis_hbm.at[pl.ds(k * VIS_CHUNK, VIS_CHUNK)],
            vis_buf.at[pl.ds(k * VIS_CHUNK, VIS_CHUNK)],
            vis_sems.at[k],
        )
        for k in range(CHUNKS)
    ]
    for copy in loads[:5] + vis_loads + loads[5:]:
        copy.start()

    barrier = pltpu.get_barrier_semaphore()

    @pl.loop(1, DEVICES)
    def _(k):
        other = lax.rem(me + k, DEVICES)
        pl.semaphore_signal(barrier, inc=1, device_id={"vis": other}, device_id_type=MESH)

    def remote(src, dst, send, recv, other):
        return pltpu.make_async_remote_copy(
            src_ref=src, dst_ref=dst, send_sem=send, recv_sem=recv,
            device_id={"vis": other}, device_id_type=MESH,
        )

    def wait_for(ref, sem):
        pltpu.make_async_copy(ref, ref, sem).wait()

    def to_all(piece, place, index):
        @pl.loop(1, DEVICES)
        def _(k):
            other = lax.rem(me + k, DEVICES)
            remote(piece(other), place, send_sems.at[index], recv_sems.at[index], other).start()

        pltpu.make_async_copy(piece(me), place, recv_sems.at[index]).start()

    def exchange_columns(stage):
        def piece(other):
            f, _, c = owner(other)
            return half_buf.at[
                stage,
                pl.ds(pl.multiple_of(f * ROWS, ROWS), ROWS),
                pl.ds(pl.multiple_of(c * WIDE, WIDE), WIDE),
            ]

        to_all(piece, column_buf.at[stage, me], 2 * stage)

    def exchange_rows(stage):
        def piece(other):
            return u_buf.at[stage, pl.ds(pl.multiple_of(other * ROWS, ROWS), ROWS), :]

        place = row_in.at[
            stage, column * 2 + row_block, pl.ds(pl.multiple_of(facet * ROWS, ROWS), ROWS), :
        ]
        to_all(piece, place, 2 * stage + 1)

    for copy in loads[:4]:
        copy.wait()

    lane = lax.broadcasted_iota(jnp.int32, (1, S), 1)
    tile = lax.broadcasted_iota(jnp.int32, (TILE_CAP, S), 0)
    slot_row = jnp.full((1, S), SLOTS, jnp.int32)
    plane_row = jnp.full((1, S), WPLANES, jnp.int32)
    slot_column = jnp.full((TILE_CAP, S), SLOTS, jnp.int32)
    for t in range(TILE_CAP):
        patch = patch_ref[t]
        slot = facet_ref[t] * NP + lax.rem(patch, 4) * 4 + lax.div(patch, 4)
        slot = jnp.where(t < count_ref[0], slot, SLOTS)
        slot_row = jnp.where(lane == t, slot, slot_row)
        plane_row = jnp.where(lane == t, plane_ref[t], plane_row)
        slot_column = jnp.where(tile == t, slot, slot_column)
    tile_lane = lax.broadcasted_iota(jnp.int32, (TILE_CAP, S), 1)
    before = jnp.max(
        jnp.where((slot_column == slot_row) & (tile_lane < tile), tile_lane, -1), axis=1, keepdims=True
    )
    slot_lane = lax.broadcasted_iota(jnp.int32, (SLOTS, S), 1)
    member = lax.broadcasted_iota(jnp.int32, (SLOTS, S), 0) == slot_row
    last = jnp.max(jnp.where(member, slot_lane, -1), axis=1, keepdims=True)
    before = jnp.where(before < 0, TILE_CAP, before)
    last = jnp.where(last < 0, TILE_CAP, last)

    in_plane = jnp.where(
        lax.broadcasted_iota(jnp.int32, (WPLANES, S), 0) == plane_row, 1.0, 0.0
    )
    in_slot = jnp.where(member, 1.0, 0.0)
    held = []
    for device in range(DEVICES):
        f, r, c = static_owner(device)
        held += [slot_of(f, r, c), slot_of(f, 3 - r, 3 - c)]
    pairs = stack(*[(in_plane * in_slot[s:s + 1, :]).astype(BF16) for s in held])
    cnt_out[...] = dot(pairs, jnp.ones((S, S), BF16)).astype(BF16).reshape(DEVICES, 2, WPLANES, S)

    loads[4].wait()

    @pl.loop(0, WPLANES)
    def _(w):
        real, imag = w_ref[w, 0], w_ref[w, 1]
        back_op[w] = lanes(real.T, imag.T)
        term_op[w] = stack(lanes(real, -imag), lanes(imag, real))

    run_buf[TILE_CAP] = jnp.zeros((S, 2 * S), F32)
    for k in range(CHUNKS):
        vis_loads[k].wait()
        for t in range(k * VIS_CHUNK, (k + 1) * VIS_CHUNK):
            plane = plane_ref[t]
            real, imag = vis_buf[t, 0], vis_buf[t, 1]
            half = dot(lanes(real, imag), term_op[plane])
            half_real, half_imag = half[:, :S].astype(BF16), half[:, S:].astype(BF16)
            term = dot(
                back_op[plane], stack(lanes(half_real, half_imag), lanes(half_imag, -half_real))
            )
            run_buf[t] = term + run_buf[before[t, 0]]

    loads[5].wait()
    loads[7].wait()
    row = lax.broadcasted_iota(jnp.int32, (S, P_SIZE), 0)
    for c in range(4):
        at, low, edge = c * WIDE, c * S, (c + 1) % 4 * S
        to_cols[:, at:at + S] = cs_ref[0, :, low:low + S]
        to_cols[:, at + S:at + 2 * S] = -cs_ref[1, :, low:low + S]
        to_cols[:, at + 2 * S:at + WIDE] = edge_ref[:, low:low + S]
        to_rows[at:at + S, :] = cs_ref[0, low:low + S, :]
        to_rows[at + S:at + 2 * S, :] = -cs_ref[1, low:low + S, :]
        cosine_row = cs_ref[0, edge:edge + 1, :].astype(F32)
        sine_row = cs_ref[1, edge:edge + 1, :].astype(F32)
        to_rows[at + 2 * S:at + WIDE, :] = jnp.where(
            row == 0, cosine_row, jnp.where(row == 1, -sine_row, 0.0)
        ).astype(BF16)
    loads[6].wait()
    half_buf[0] = dot(sky_ref[0], to_cols[...]).astype(BF16)

    mirror_rows = where_equal(
        (S, 2 * S), lambda i, k: one_if(((k == S - i) & (i > 0)) | ((k == S) & (i == 0)))
    )
    mirror_cols = where_equal(
        (2 * S, S), lambda k, j: one_if(((k == S - j) & (j > 0)) | ((k == S) & (j == 0)))
    )
    far_cols = where_equal(
        (2 * S, S), lambda k, j: one_if(((k == S - j) & (j > 0)) | ((k == S + 1) & (j == 0)))
    )
    near_spread = where_equal(
        (S, 2 * S), lambda j, k: one_if(((k == S - j) & (j > 0)) | ((k == S) & (j == 0)))
    )
    far_spread = where_equal(
        (S, 2 * S), lambda j, k: one_if(((k == S - j) & (j > 0)) | ((k == S + 1) & (j == 0)))
    )
    unfold_rows = where_equal((S, EXT), lambda i, k: one_if(k == S - i))
    fold_rows = where_equal((EXT, S), lambda k, i: one_if(k == S - i))
    quarter_turn = where_equal(
        (S, S), lambda i, j: one_if((i == 0) & (j == 1)) - one_if((i == 1) & (j == 0))
    )
    pick_ends = where_equal(
        (ROWS, 2 * S), lambda i, k: one_if(((i == 0) & (k == 0)) | ((i == 1) & (k == S)))
    )
    put_real = where_equal((ROWS, S), lambda i, j: one_if((i == 1) & (j == 0)))
    put_imag = where_equal((ROWS, S), lambda i, j: one_if((i == 1) & (j == 1)))

    def contract(a, b, dims):
        return lax.dot_general(a, b, (dims, ((), ())), preferred_element_type=F32)

    @pl.loop(0, WPLANES)
    def _(w):
        real, imag = w_ref[w, 0], w_ref[w, 1]
        gram = dot(back_op[w], stack(lanes(real, imag), lanes(imag, -real))).astype(BF16)
        gram_real, gram_imag = gram[:, :S], gram[:, S:]
        left_op[pl.ds(w * S, S), :] = gram
        right_op[pl.ds(w * 2 * S, S), :] = lanes(gram_real, -gram_imag)
        right_op[pl.ds(w * 2 * S + S, S), :] = lanes(gram_imag, gram_real)

    pl.semaphore_wait(barrier, DEVICES - 1)
    to_all(lambda other: cnt_out.at[other], cnt_in.at[me], 4)
    exchange_columns(0)

    def first_stage(f):
        for k in range(1, 4):
            if f < 2:
                step = lax.rem(at_x + k, 4)
                other = at_z * 16 + at_y * 4 + step
            else:
                step = lax.rem(at_y + k, 4)
                other = at_z * 16 + step * 4 + at_x
            remote(
                first_out.at[f, :, step], first_in.at[f, k - 1], dirty_send.at[0, f], dirty_recv.at[0, f], other
            ).start()

    def second_stage(group):
        for f in (2 * group, 2 * group + 1):
            wait_for(first_in.at[f], dirty_recv.at[0, f])
            total = first_out[f, :, at_x if group == 0 else at_y].astype(F32)
            for k in range(3):
                total += first_in[f, k].astype(F32)
            second_out[group, 2 * (f % 2):2 * (f % 2) + 2] = total.astype(BF16)
        for k in range(1, 4):
            if group == 0:
                step = lax.rem(at_y + k, 4)
                other = at_z * 16 + step * 4 + at_x
            else:
                step = lax.rem(at_x + k, 4)
                other = at_z * 16 + at_y * 4 + step
            remote(
                second_out.at[group, step], second_in.at[group, k - 1],
                dirty_send.at[1, group], dirty_recv.at[1, group], other,
            ).start()

    def third_sum(group):
        wait_for(second_in.at[group], dirty_recv.at[1, group])
        total = second_out[group, at_y if group == 0 else at_x].astype(F32)
        for k in range(3):
            total += second_in[group, k].astype(F32)
        third_own[group] = total

    def third_stage():
        third_out[...] = third_own[1 - at_z].astype(BF16)
        remote(
            third_out, third_in, dirty_send.at[2, 0], dirty_recv.at[2, 0], lax.rem(me + 16, DEVICES)
        ).start()

    def hermitian_rows(f):
        for s in range(NP):
            grid_buf[s] = run_buf[last[f * NP + s, 0]].astype(BF16)

        def mirrored(r, c):
            return dot(mirror_rows, stack(grid_buf[c * 4 + 3 - r], grid_buf[c * 4 + (4 - r) % 4])).astype(BF16)

        def folded(own, rows, c):
            near, edge = rows[3 - c], rows[(4 - c) % 4]
            real = dot(lanes(near[:, :S], edge[:, :S]), mirror_cols)
            imag = dot(lanes(near[:, S:], edge[:, S:]), mirror_cols)
            return own.astype(F32) + lanes(real, -imag)

        middle = [grid_buf[c * 4 + 2, 0:ROWS, :] for c in range(4)]
        last_rows = [folded(middle[c], middle, c) for c in range(4)]
        blocks = []
        for r in range(2):
            rows = [mirrored(r, c) for c in range(4)]
            blocks.append([folded(grid_buf[c * 4 + r], rows, c).astype(BF16) for c in range(4)])
        tail_row = lax.broadcasted_iota(jnp.int32, (ROWS, 2 * S), 0)
        for r in range(2):
            next_rows = [blocks[1][c][0:ROWS].astype(F32) if r == 0 else last_rows[c] for c in range(4)]
            for c in range(4):
                after = (c + 1) % 4
                ends = contract(pick_ends, blocks[r][after], ((1,), (1,)))
                tail = jnp.where(
                    tail_row == 0, next_rows[c][0:1, :],
                    jnp.where(
                        tail_row == 1, lanes(ends[0:1, :], ends[1:2, :]),
                        jnp.where(tail_row == 2, next_rows[after][0:1, :], 0.0),
                    ),
                )
                first_out[f, r, c, 0:S, :] = blocks[r][c]
                first_out[f, r, c, S:EXT, :] = tail.astype(BF16)

    for f in (0, 2, 1, 3):
        hermitian_rows(f)
        first_stage(f)

    wait_for(cnt_in, recv_sems.at[4])
    counts = jnp.sum(cnt_in[...].astype(F32), axis=0)

    low = pl.multiple_of(row_block * S, S)

    def model_grid(stage):
        wait_for(column_buf.at[stage], recv_sems.at[2 * stage])
        half = column_buf[stage].reshape(P_SIZE, WIDE)
        edge = dot(half[:, 2 * S:], quarter_turn).astype(BF16)
        turned = lanes(half[:, S:2 * S], -half[:, :S], -edge)
        return dot(cs_ref[0, pl.ds(low, EXT), :], half) + dot(cs_ref[1, pl.ds(low, EXT), :], turned)

    def slot_model(grid):
        first = grid[:S, :2 * S]
        rows = dot(unfold_rows, grid).astype(BF16)
        second = lanes(
            dot(lanes(rows[:, :S], rows[:, 2 * S:]), mirror_cols),
            -dot(lanes(rows[:, S:2 * S], rows[:, 2 * S:]), far_cols),
        ).astype(BF16)
        for q, patch in enumerate((first, second)):
            operand = stack(patch, lanes(-patch[:, S:], patch[:, :S]))
            for w in range(WPLANES):
                part = dot(left_op[w * S:(w + 1) * S, :], operand)
                scale = counts[q, w:w + 1, :]
                b_buf[q * S:(q + 1) * S, w * 2 * S:(w + 1) * 2 * S] = (part * lanes(scale, scale)).astype(BF16)
        model = dot(b_buf[...], right_op[...])
        rows = dot(fold_rows, model[S:].astype(BF16)).astype(BF16)
        real, imag = dot(rows[:, :S], near_spread), dot(rows[:, S:], far_spread)
        mirrored = lanes(real[:, :S], -imag[:, :S], real[:, S:] - imag[:, S:])
        own = stack(lanes(model[:S], jnp.zeros((S, S), F32)), jnp.zeros((ROWS, WIDE), F32))
        return own + mirrored

    spread_buf[EXT:, :] = jnp.zeros((2 * S - EXT, WIDE), BF16)
    turn_pad = jnp.zeros((2 * S - EXT, WIDE), BF16)

    def column_transform(stage, values):
        values = values.astype(BF16)
        edge = dot(values[:, 2 * S:], quarter_turn).astype(BF16)
        turned = stack(lanes(-values[:, S:2 * S], values[:, :S], edge), turn_pad)
        spread_buf[:EXT, :] = values
        u_buf[stage] = (
            dot(cs_ref[0, :, pl.ds(low, 2 * S)], spread_buf[...]) + dot(cs_ref[1, :, pl.ds(low, 2 * S)], turned)
        ).astype(BF16)
        exchange_rows(stage)

    def image_rows(stage):
        wait_for(row_in.at[stage], recv_sems.at[2 * stage + 1])
        parts = [
            (row_in[stage, 2 * c].astype(F32) + row_in[stage, 2 * c + 1].astype(F32)).astype(BF16)
            for c in range(4)
        ]
        return dot(lanes(*parts), to_rows[...])

    column_transform(0, slot_model(model_grid(0).astype(BF16)))
    second_stage(0)
    second_stage(1)
    sky = (sky_ref[1].astype(F32) - (LOOP_GAIN * WEIGHT) * image_rows(0)).astype(BF16)
    half_buf[1] = dot(sky, to_cols[...]).astype(BF16)
    third_sum(0)
    third_sum(1)
    third_stage()
    exchange_columns(1)
    grid = model_grid(1)
    wait_for(third_in, dirty_recv.at[2, 0])
    dirty = third_own[at_z] + third_in[...].astype(F32)
    tail = dirty[S:].astype(BF16)
    ends = contract(tail[:, :S], put_real, ((0,), (0,))) + contract(tail[:, S:], put_imag, ((0,), (0,)))
    corner_row = lax.broadcasted_iota(jnp.int32, (ROWS, S), 0)
    corner_lane = lax.broadcasted_iota(jnp.int32, (ROWS, S), 1)
    corner = jnp.where(
        corner_row > 0, 0.0,
        jnp.where(
            corner_lane == 0, dirty[S + 2:S + 3, 0:1],
            jnp.where(corner_lane == 1, dirty[S + 2:S + 3, S:S + 1], 0.0),
        ),
    )
    grid += (0.5 * LOOP_GAIN * WEIGHT) * lanes(dirty, stack(ends, corner))
    model = slot_model(grid.astype(BF16))
    ext_row = lax.broadcasted_iota(jnp.int32, (EXT, 2 * S), 0)
    share = jnp.where(
        ext_row == 0, jnp.where(row_block == 0, 0.5, 1.0),
        jnp.where(ext_row < S, 1.0, jnp.where((ext_row == S) & (row_block == 1), 0.5, 0.0)),
    )
    column_transform(1, lanes(dirty * share - model[:, :2 * S], -model[:, 2 * S:]))
    out_ref[...] = image_rows(1) * WEIGHT

    for stage in range(2):
        wait_for(column_buf.at[stage, pl.ds(0, DEVICES - 1)], send_sems.at[2 * stage])
        wait_for(u_buf.at[stage, pl.ds(0, P_SIZE - ROWS), :], send_sems.at[2 * stage + 1])
    wait_for(cnt_in.at[pl.ds(0, DEVICES - 1)], send_sems.at[4])
    for f in range(F):
        wait_for(first_in.at[f], dirty_send.at[0, f])
    for group in range(2):
        wait_for(second_in.at[group], dirty_send.at[1, group])
    wait_for(third_in, dirty_send.at[2, 0])


def imaging(*operands):
    hbm = pl.BlockSpec(memory_space=pltpu.HBM)
    return pl.pallas_call(
        imaging_kernel,
        out_shape=jax.ShapeDtypeStruct((F * ROWS, P_SIZE), F32),
        in_specs=[hbm] * 9,
        out_specs=pl.BlockSpec(memory_space=pltpu.VMEM),
        scratch_shapes=[
            pltpu.SMEM((TILE_CAP,), jnp.int32),
            pltpu.SMEM((TILE_CAP,), jnp.int32),
            pltpu.SMEM((TILE_CAP,), jnp.int32),
            pltpu.SMEM((1,), jnp.int32),
            pltpu.VMEM((2, F * ROWS, P_SIZE), BF16),
            pltpu.VMEM((2, P_SIZE, P_SIZE), BF16),
            pltpu.VMEM((P_SIZE, P_SIZE), BF16),
            pltpu.VMEM((WPLANES, 2, S, S), BF16),
            pltpu.VMEM((TILE_CAP, 2, S, S), BF16),
            pltpu.VMEM((WPLANES, S, 2 * S), BF16),
            pltpu.VMEM((WPLANES, 2 * S, 2 * S), BF16),
            pltpu.VMEM((TILE_CAP + 1, S, 2 * S), F32),
            pltpu.VMEM((NP, S, 2 * S), BF16),
            pltpu.VMEM((4 * WIDE, P_SIZE), BF16),
            pltpu.VMEM((P_SIZE, 4 * WIDE), BF16),
            pltpu.VMEM((2, F * ROWS, 4 * WIDE), BF16),
            pltpu.VMEM((2, DEVICES, ROWS, WIDE), BF16),
            pltpu.VMEM((2, P_SIZE, WIDE), BF16),
            pltpu.VMEM((2, 8, F * ROWS, WIDE), BF16),
            pltpu.VMEM((DEVICES, 2, WPLANES, S), BF16),
            pltpu.VMEM((DEVICES, 2, WPLANES, S), BF16),
            pltpu.VMEM((WPLANES * S, 2 * S), BF16),
            pltpu.VMEM((WPLANES * 2 * S, 2 * S), BF16),
            pltpu.VMEM((2 * S, WPLANES * 2 * S), BF16),
            pltpu.VMEM((2 * S, WIDE), BF16),
            pltpu.VMEM((F, 2, 4, EXT, 2 * S), BF16),
            pltpu.VMEM((F, 3, 2, EXT, 2 * S), BF16),
            pltpu.VMEM((2, 4, EXT, 2 * S), BF16),
            pltpu.VMEM((2, 3, EXT, 2 * S), BF16),
            pltpu.VMEM((2, EXT, 2 * S), F32),
            pltpu.VMEM((EXT, 2 * S), BF16),
            pltpu.VMEM((EXT, 2 * S), BF16),
            pltpu.SemaphoreType.DMA((8,)),
            pltpu.SemaphoreType.DMA((CHUNKS,)),
            pltpu.SemaphoreType.DMA((5,)),
            pltpu.SemaphoreType.DMA((5,)),
            pltpu.SemaphoreType.DMA((3, F)),
            pltpu.SemaphoreType.DMA((3, F)),
        ],
        compiler_params=pltpu.CompilerParams(
            collective_id=0, has_side_effects=True, vmem_limit_bytes=56 << 20
        ),
        name="imaging",
    )(*operands)


def dft_tables():
    phases = np.outer(np.arange(P_SIZE), np.arange(P_SIZE)) % P_SIZE
    angles = phases * (2.0 * math.pi / P_SIZE)
    tables = np.stack([np.cos(angles), np.sin(angles)]) / math.sqrt(P_SIZE)
    edges = np.zeros((P_SIZE, 4, S))
    for c in range(4):
        edges[:, c, 0] = tables[0, :, (c + 1) % 4 * S]
        edges[:, c, 1] = -tables[1, :, (c + 1) % 4 * S]
    return tables.astype(BF16), edges.reshape(P_SIZE, P_SIZE).astype(BF16)


def local(model_input, w_kernels, visibilities, tile_facet, tile_patch, tile_wplane, tile_count):
    sky = model_input.reshape(2, F * ROWS, P_SIZE)
    cosines, edges = dft_tables()
    image = imaging(
        tile_facet, tile_patch, tile_wplane, tile_count,
        sky, jnp.asarray(cosines), jnp.asarray(edges), w_kernels, visibilities,
    )
    return image.reshape(F, ROWS, P_SIZE)


def solution(mesh):
    return jax.shard_map(
        local,
        mesh=mesh,
        in_specs=(
            P(None, "freq", "vis", None),
            P("freq", None, None, None),
            P(("freq", "vis"), None, None, None),
            P(("freq", "vis")),
            P(("freq", "vis")),
            P(("freq", "vis")),
            P(("freq", "vis")),
        ),
        out_specs=P("freq", "vis", None),
        check_vma=False,
    )
```

time: 61.3 us -> 65.5 us (1.069)
  Pallas kernels: 58.9 us -> 63 us
    pallas_call x1, Pallas kernels: 58.9 us -> 63 us  [imaging(): pl.pallas_call(imaging_kernel, out_shape=jax.ShapeDtypeStruct((F * ROWS,...]
where the time goes in v3:
time: 65.5 us; the launch traced here: 65.2 us
  Pallas kernels  63 us (96%)
  local copies, waits for them, and re-layouts  1.57 us (2%)
  between operations  0.66 us (1%)
    pallas_call x1, Pallas kernels, imaging(): pl.pallas_call(imaging_kernel, out_shape=jax.ShapeDtypeStruct((F * ROWS,...  63 us
    unnamed x1, local copies, waits for them, and re-layouts  1.57 us

profile of v3, /device:TPU:0, one launch (start us, length us, event | category | flops | bytes accessed | tf_op | source)
XLA Modules:
  0.0 65.2 jit_solution(144640181291965408)
XLA Ops:
  0.7 63.0 %imaging.1 = f32[64,512]{1,0:T(8,128)} custom-call(s32[32]{0:T(128)} %facet_hbm.1, s32[32]{0:T(128)} %patch_hbm.1, s32[32]{0:T(128)} %plane_hbm.1, s32[1]{0:T(128)S(6)} %copy.11.count_hbm, bf16[2,64,512]{2,1,0:T(8,128)(2,1)} %bitcast.3, bf16[2,512,512]{2,1,0:T(8,128)(2,1)} %constant.4.clone.cs_hbm, bf16[512,512]{1,0:T(8,128)(2,1)} %constant.5.clone.edge_hbm, ...), custom_call_target="tpu_custom_call" | custom-call | tf_op jit(solution)/shard_map/imaging/pallas_call | solution.py:445
  63.6 1.6 %copy.12 = f32[4,16,512]{2,1,0:T(8,128)} copy(f32[4,16,512]{2,1,0:T(8,128)} %bitcast.2) | data formatting | bytes 262144

commit v4 on v3

--- a/solution.py
+++ b/solution.py
@@ -71,9 +71,9 @@
     facet_hbm, patch_hbm, plane_hbm, count_hbm, sky_hbm, cs_hbm, edge_hbm, w_hbm, vis_hbm, out_ref,
     facet_ref, patch_ref, plane_ref, count_ref, sky_ref, cs_ref, edge_ref, w_ref, vis_buf,
     back_op, term_op, run_buf, grid_buf, to_rows, to_cols, half_buf, column_buf, u_buf, row_in,
-    cnt_out, cnt_in, left_op, right_op, b_buf, spread_buf,
+    cnt_buf, left_op, right_op, b_buf, spread_buf,
     first_out, first_in, second_out, second_in, third_own, third_out, third_in,
-    load_sems, vis_sems, send_sems, recv_sems, dirty_send, dirty_recv,
+    fold_buf, last_ref, load_sems, vis_sems, plane_sem, group_sem, send_sems, recv_sems, dirty_send, dirty_recv,
 ):
     me = lax.axis_index("vis")
     facet, row_block, column = owner(me)
@@ -101,10 +101,15 @@
 
     barrier = pltpu.get_barrier_semaphore()
 
-    @pl.loop(1, DEVICES)
-    def _(k):
-        other = lax.rem(me + k, DEVICES)
-        pl.semaphore_signal(barrier, inc=1, device_id={"vis": other}, device_id_type=MESH)
+    along_x = [at_z * 16 + at_y * 4 + lax.rem(at_x + k, 4) for k in range(1, 4)]
+    along_y = [at_z * 16 + lax.rem(at_y + k, 4) * 4 + at_x for k in range(1, 4)]
+    across = lax.rem(me + 16, DEVICES)
+
+    def tell(semaphore, others):
+        for other in others:
+            pl.semaphore_signal(semaphore, inc=1, device_id={"vis": other}, device_id_type=MESH)
+
+    tell(barrier, along_x + along_y + [across])
 
     def remote(src, dst, send, recv, other):
         return pltpu.make_async_remote_copy(
@@ -124,24 +129,24 @@
         pltpu.make_async_copy(piece(me), place, recv_sems.at[index]).start()
 
     def exchange_columns(stage):
+        width = WIDE - stage * S
+
         def piece(other):
             f, _, c = owner(other)
             return half_buf.at[
                 stage,
                 pl.ds(pl.multiple_of(f * ROWS, ROWS), ROWS),
-                pl.ds(pl.multiple_of(c * WIDE, WIDE), WIDE),
+                pl.ds(pl.multiple_of(c * WIDE, S), width),
             ]
 
-        to_all(piece, column_buf.at[stage, me], 2 * stage)
-
-    def exchange_rows(stage):
+        to_all(piece, column_buf.at[stage, me, :, pl.ds(0, width)], 2 * stage)
+
+    def exchange_rows():
         def piece(other):
-            return u_buf.at[stage, pl.ds(pl.multiple_of(other * ROWS, ROWS), ROWS), :]
-
-        place = row_in.at[
-            stage, column * 2 + row_block, pl.ds(pl.multiple_of(facet * ROWS, ROWS), ROWS), :
-        ]
-        to_all(piece, place, 2 * stage + 1)
+            return u_buf.at[pl.ds(pl.multiple_of(other * ROWS, ROWS), ROWS), :]
+
+        place = row_in.at[column * 2 + row_block, pl.ds(pl.multiple_of(facet * ROWS, ROWS), ROWS), :]
+        to_all(piece, place, 1)
 
     for copy in loads[:4]:
         copy.wait()
@@ -167,17 +172,26 @@
     last = jnp.max(jnp.where(member, slot_lane, -1), axis=1, keepdims=True)
     before = jnp.where(before < 0, TILE_CAP, before)
     last = jnp.where(last < 0, TILE_CAP, last)
+    for s in range(SLOTS):
+        last_ref[s] = last[s, 0]
 
     in_plane = jnp.where(
         lax.broadcasted_iota(jnp.int32, (WPLANES, S), 0) == plane_row, 1.0, 0.0
     )
     in_slot = jnp.where(member, 1.0, 0.0)
-    held = []
-    for device in range(DEVICES):
-        f, r, c = static_owner(device)
-        held += [slot_of(f, r, c), slot_of(f, 3 - r, 3 - c)]
-    pairs = stack(*[(in_plane * in_slot[s:s + 1, :]).astype(BF16) for s in held])
-    cnt_out[...] = dot(pairs, jnp.ones((S, S), BF16)).astype(BF16).reshape(DEVICES, 2, WPLANES, S)
+    in_plane = in_plane.astype(BF16)
+    lane_row = lax.broadcasted_iota(jnp.int32, (S, S), 0)
+
+    def contract(a, b, dims):
+        return lax.dot_general(a, b, (dims, ((), ())), preferred_element_type=F32)
+
+    for f in range(F):
+        for c in range(4):
+            match = jnp.zeros((S, S), F32)
+            for k, (r, q) in enumerate(((0, 0), (0, 1), (1, 0), (1, 1))):
+                s = slot_of(f, 3 - r, 3 - c) if q else slot_of(f, r, c)
+                match = jnp.where(lane_row == 4 + k, in_slot[s:s + 1, :], match)
+            cnt_buf[f * ROWS:(f + 1) * ROWS, c * S:(c + 1) * S] = contract(in_plane, match.astype(BF16), ((1,), (1,)))
 
     loads[4].wait()
 
@@ -199,24 +213,26 @@
                 back_op[plane], stack(lanes(half_real, half_imag), lanes(half_imag, -half_real))
             )
             run_buf[t] = term + run_buf[before[t, 0]]
+        if k == CHUNKS // 2 - 1:
+            pl.semaphore_wait(barrier, 7)
+            tell(plane_sem, along_y)
+    pl.semaphore_wait(plane_sem, 3)
+    tell(group_sem, [across])
 
     loads[5].wait()
     loads[7].wait()
-    row = lax.broadcasted_iota(jnp.int32, (S, P_SIZE), 0)
     for c in range(4):
-        at, low, edge = c * WIDE, c * S, (c + 1) % 4 * S
+        at, low = c * 2 * S, c * S
         to_cols[:, at:at + S] = cs_ref[0, :, low:low + S]
         to_cols[:, at + S:at + 2 * S] = -cs_ref[1, :, low:low + S]
-        to_cols[:, at + 2 * S:at + WIDE] = edge_ref[:, low:low + S]
-        to_rows[at:at + S, :] = cs_ref[0, low:low + S, :]
-        to_rows[at + S:at + 2 * S, :] = -cs_ref[1, low:low + S, :]
-        cosine_row = cs_ref[0, edge:edge + 1, :].astype(F32)
-        sine_row = cs_ref[1, edge:edge + 1, :].astype(F32)
-        to_rows[at + 2 * S:at + WIDE, :] = jnp.where(
-            row == 0, cosine_row, jnp.where(row == 1, -sine_row, 0.0)
-        ).astype(BF16)
     loads[6].wait()
-    half_buf[0] = dot(sky_ref[0], to_cols[...]).astype(BF16)
+    for cycle in range(2):
+        half = dot(sky_ref[cycle], to_cols[...])
+        for c in range(4):
+            half_buf[cycle, :, c * WIDE:c * WIDE + 2 * S] = half[:, c * 2 * S:(c + 1) * 2 * S].astype(BF16)
+    extra = cnt_buf[...] + dot(sky_ref[0], edge_ref[...]) + pltpu.roll(dot(sky_ref[1], edge_ref[...]), 2, 1)
+    for c in range(4):
+        half_buf[0, :, c * WIDE + 2 * S:(c + 1) * WIDE] = extra[:, c * S:(c + 1) * S].astype(BF16)
 
     mirror_rows = where_equal(
         (S, 2 * S), lambda i, k: one_if(((k == S - i) & (i > 0)) | ((k == S) & (i == 0)))
@@ -241,35 +257,20 @@
     pick_ends = where_equal(
         (ROWS, 2 * S), lambda i, k: one_if(((i == 0) & (k == 0)) | ((i == 1) & (k == S)))
     )
+    pick_edge = [
+        where_equal((S, S), lambda i, j: one_if((i == 2 * cycle + j) & (j < 2))) for cycle in range(2)
+    ]
     put_real = where_equal((ROWS, S), lambda i, j: one_if((i == 1) & (j == 0)))
     put_imag = where_equal((ROWS, S), lambda i, j: one_if((i == 1) & (j == 1)))
 
-    def contract(a, b, dims):
-        return lax.dot_general(a, b, (dims, ((), ())), preferred_element_type=F32)
-
-    @pl.loop(0, WPLANES)
-    def _(w):
-        real, imag = w_ref[w, 0], w_ref[w, 1]
-        gram = dot(back_op[w], stack(lanes(real, imag), lanes(imag, -real))).astype(BF16)
-        gram_real, gram_imag = gram[:, :S], gram[:, S:]
-        left_op[pl.ds(w * S, S), :] = gram
-        right_op[pl.ds(w * 2 * S, S), :] = lanes(gram_real, -gram_imag)
-        right_op[pl.ds(w * 2 * S + S, S), :] = lanes(gram_imag, gram_real)
-
-    pl.semaphore_wait(barrier, DEVICES - 1)
-    to_all(lambda other: cnt_out.at[other], cnt_in.at[me], 4)
-    exchange_columns(0)
-
     def first_stage(f):
+        turn = lax.div(f, 2)
         for k in range(1, 4):
-            if f < 2:
-                step = lax.rem(at_x + k, 4)
-                other = at_z * 16 + at_y * 4 + step
-            else:
-                step = lax.rem(at_y + k, 4)
-                other = at_z * 16 + step * 4 + at_x
+            step = lax.rem(at_x + turn * (at_y - at_x) + k, 4)
+            x, y = at_x + (1 - turn) * (step - at_x), at_y + turn * (step - at_y)
             remote(
-                first_out.at[f, :, step], first_in.at[f, k - 1], dirty_send.at[0, f], dirty_recv.at[0, f], other
+                first_out.at[f, :, step], first_in.at[f, k - 1], dirty_send.at[0, f], dirty_recv.at[0, f],
+                at_z * 16 + y * 4 + x,
             ).start()
 
     def second_stage(group):
@@ -304,9 +305,12 @@
             third_out, third_in, dirty_send.at[2, 0], dirty_recv.at[2, 0], lax.rem(me + 16, DEVICES)
         ).start()
 
-    def hermitian_rows(f):
+    def hermitian_rows(f, model=None):
         for s in range(NP):
-            grid_buf[s] = run_buf[last[f * NP + s, 0]].astype(BF16)
+            grid_buf[s] = run_buf[last_ref[f * NP + s]].astype(BF16)
+        if model is not None:
+            for q, s in enumerate((column * 4 + row_block, (3 - column) * 4 + 3 - row_block)):
+                grid_buf[s] = (run_buf[last_ref[f * NP + s]] - model[q * S:(q + 1) * S]).astype(BF16)
 
         def mirrored(r, c):
             return dot(mirror_rows, stack(grid_buf[c * 4 + 3 - r], grid_buf[c * 4 + (4 - r) % 4])).astype(BF16)
@@ -339,21 +343,33 @@
                 first_out[f, r, c, 0:S, :] = blocks[r][c]
                 first_out[f, r, c, S:EXT, :] = tail.astype(BF16)
 
-    for f in (0, 2, 1, 3):
+    turn, part = lax.div(facet, 2), lax.rem(facet, 2)
+    others = (2 * (1 - turn) + part, 2 * turn + 1 - part, 2 * (1 - turn) + 1 - part)
+    pl.semaphore_wait(group_sem, 1)
+    exchange_columns(0)
+    exchange_columns(1)
+    for f in others:
         hermitian_rows(f)
         first_stage(f)
 
-    wait_for(cnt_in, recv_sems.at[4])
-    counts = jnp.sum(cnt_in[...].astype(F32), axis=0)
+    @pl.loop(0, WPLANES)
+    def _(w):
+        real, imag = w_ref[w, 0], w_ref[w, 1]
+        gram = dot(back_op[w], stack(lanes(real, imag), lanes(imag, -real))).astype(BF16)
+        gram_real, gram_imag = gram[:, :S], gram[:, S:]
+        left_op[pl.ds(w * S, S), :] = gram
+        right_op[pl.ds(w * 2 * S, S), :] = lanes(gram_real, -gram_imag)
+        right_op[pl.ds(w * 2 * S + S, S), :] = lanes(gram_imag, gram_real)
 
     low = pl.multiple_of(row_block * S, S)
 
     def model_grid(stage):
-        wait_for(column_buf.at[stage], recv_sems.at[2 * stage])
-        half = column_buf[stage].reshape(P_SIZE, WIDE)
-        edge = dot(half[:, 2 * S:], quarter_turn).astype(BF16)
-        turned = lanes(half[:, S:2 * S], -half[:, :S], -edge)
-        return dot(cs_ref[0, pl.ds(low, EXT), :], half) + dot(cs_ref[1, pl.ds(low, EXT), :], turned)
+        half = column_buf[stage, :, :, 0:2 * S].reshape(P_SIZE, 2 * S)
+        extra = column_buf[0, :, :, 2 * S:].reshape(P_SIZE, S)
+        edge = dot(extra, pick_edge[stage]).astype(BF16)
+        edge_turned = dot(edge, quarter_turn).astype(BF16)
+        turned = lanes(half[:, S:], -half[:, :S], -edge_turned)
+        return dot(cs_ref[0, pl.ds(low, EXT), :], lanes(half, edge)) + dot(cs_ref[1, pl.ds(low, EXT), :], turned)
 
     def slot_model(grid):
         first = grid[:S, :2 * S]
@@ -366,46 +382,59 @@
             operand = stack(patch, lanes(-patch[:, S:], patch[:, :S]))
             for w in range(WPLANES):
                 part = dot(left_op[w * S:(w + 1) * S, :], operand)
-                scale = counts[q, w:w + 1, :]
-                b_buf[q * S:(q + 1) * S, w * 2 * S:(w + 1) * 2 * S] = (part * lanes(scale, scale)).astype(BF16)
+                b_buf[q * S:(q + 1) * S, w * 2 * S:(w + 1) * 2 * S] = (part * counts[w:w + 1, q:q + 1]).astype(BF16)
         model = dot(b_buf[...], right_op[...])
         rows = dot(fold_rows, model[S:].astype(BF16)).astype(BF16)
         real, imag = dot(rows[:, :S], near_spread), dot(rows[:, S:], far_spread)
         mirrored = lanes(real[:, :S], -imag[:, :S], real[:, S:] - imag[:, S:])
         own = stack(lanes(model[:S], jnp.zeros((S, S), F32)), jnp.zeros((ROWS, WIDE), F32))
-        return own + mirrored
+        return model, own + mirrored
 
     spread_buf[EXT:, :] = jnp.zeros((2 * S - EXT, WIDE), BF16)
     turn_pad = jnp.zeros((2 * S - EXT, WIDE), BF16)
 
-    def column_transform(stage, values):
+    def column_transform(values):
         values = values.astype(BF16)
         edge = dot(values[:, 2 * S:], quarter_turn).astype(BF16)
         turned = stack(lanes(-values[:, S:2 * S], values[:, :S], edge), turn_pad)
         spread_buf[:EXT, :] = values
-        u_buf[stage] = (
+        u_buf[...] = (
             dot(cs_ref[0, :, pl.ds(low, 2 * S)], spread_buf[...]) + dot(cs_ref[1, :, pl.ds(low, 2 * S)], turned)
         ).astype(BF16)
-        exchange_rows(stage)
-
-    def image_rows(stage):
-        wait_for(row_in.at[stage], recv_sems.at[2 * stage + 1])
+        exchange_rows()
+
+    def image_rows():
+        wait_for(row_in, recv_sems.at[1])
         parts = [
-            (row_in[stage, 2 * c].astype(F32) + row_in[stage, 2 * c + 1].astype(F32)).astype(BF16)
+            (row_in[2 * c].astype(F32) + row_in[2 * c + 1].astype(F32)).astype(BF16)
             for c in range(4)
         ]
         return dot(lanes(*parts), to_rows[...])
 
-    column_transform(0, slot_model(model_grid(0).astype(BF16)))
+    wait_for(column_buf.at[0], recv_sems.at[0])
+    counts = jnp.sum(column_buf[0, :, :, 2 * S:].astype(F32), axis=0)
+    counts = jnp.where(row_block == 0, counts[:, 4:6], counts[:, 6:8])
+    model, folded_model = slot_model(model_grid(0).astype(BF16))
+    fold_buf[...] = folded_model
+    hermitian_rows(facet, model)
+    first_stage(facet)
+    row = lax.broadcasted_iota(jnp.int32, (S, P_SIZE), 0)
+    for c in range(4):
+        at, first, edge = c * WIDE, c * S, (c + 1) % 4 * S
+        to_rows[at:at + S, :] = cs_ref[0, first:first + S, :]
+        to_rows[at + S:at + 2 * S, :] = -cs_ref[1, first:first + S, :]
+        cosine_row = cs_ref[0, edge:edge + 1, :].astype(F32)
+        sine_row = cs_ref[1, edge:edge + 1, :].astype(F32)
+        to_rows[at + 2 * S:at + WIDE, :] = jnp.where(
+            row == 0, cosine_row, jnp.where(row == 1, -sine_row, 0.0)
+        ).astype(BF16)
     second_stage(0)
     second_stage(1)
-    sky = (sky_ref[1].astype(F32) - (LOOP_GAIN * WEIGHT) * image_rows(0)).astype(BF16)
-    half_buf[1] = dot(sky, to_cols[...]).astype(BF16)
+    wait_for(column_buf.at[1, :, :, pl.ds(0, 2 * S)], recv_sems.at[2])
+    grid = model_grid(1)
     third_sum(0)
     third_sum(1)
     third_stage()
-    exchange_columns(1)
-    grid = model_grid(1)
     wait_for(third_in, dirty_recv.at[2, 0])
     dirty = third_own[at_z] + third_in[...].astype(F32)
     tail = dirty[S:].astype(BF16)
@@ -420,19 +449,19 @@
         ),
     )
     grid += (0.5 * LOOP_GAIN * WEIGHT) * lanes(dirty, stack(ends, corner))
-    model = slot_model(grid.astype(BF16))
+    _, folded_model = slot_model(grid.astype(BF16))
     ext_row = lax.broadcasted_iota(jnp.int32, (EXT, 2 * S), 0)
     share = jnp.where(
         ext_row == 0, jnp.where(row_block == 0, 0.5, 1.0),
         jnp.where(ext_row < S, 1.0, jnp.where((ext_row == S) & (row_block == 1), 0.5, 0.0)),
     )
-    column_transform(1, lanes(dirty * share - model[:, :2 * S], -model[:, 2 * S:]))
-    out_ref[...] = image_rows(1) * WEIGHT
-
-    for stage in range(2):
-        wait_for(column_buf.at[stage, pl.ds(0, DEVICES - 1)], send_sems.at[2 * stage])
-        wait_for(u_buf.at[stage, pl.ds(0, P_SIZE - ROWS), :], send_sems.at[2 * stage + 1])
-    wait_for(cnt_in.at[pl.ds(0, DEVICES - 1)], send_sems.at[4])
+    model = fold_buf[...] - folded_model
+    column_transform(lanes(dirty * share + model[:, :2 * S], model[:, 2 * S:]))
+    out_ref[...] = image_rows() * WEIGHT
+
+    wait_for(column_buf.at[0, pl.ds(0, DEVICES - 1)], send_sems.at[0])
+    wait_for(column_buf.at[1, pl.ds(0, DEVICES - 1), :, pl.ds(0, 2 * S)], send_sems.at[2])
+    wait_for(u_buf.at[pl.ds(0, P_SIZE - ROWS), :], send_sems.at[1])
     for f in range(F):
         wait_for(first_in.at[f], dirty_send.at[0, f])
     for group in range(2):
@@ -462,13 +491,12 @@
             pltpu.VMEM((TILE_CAP + 1, S, 2 * S), F32),
             pltpu.VMEM((NP, S, 2 * S), BF16),
             pltpu.VMEM((4 * WIDE, P_SIZE), BF16),
-            pltpu.VMEM((P_SIZE, 4 * WIDE), BF16),
+            pltpu.VMEM((P_SIZE, 2 * P_SIZE), BF16),
             pltpu.VMEM((2, F * ROWS, 4 * WIDE), BF16),
             pltpu.VMEM((2, DEVICES, ROWS, WIDE), BF16),
-            pltpu.VMEM((2, P_SIZE, WIDE), BF16),
-            pltpu.VMEM((2, 8, F * ROWS, WIDE), BF16),
-            pltpu.VMEM((DEVICES, 2, WPLANES, S), BF16),
-            pltpu.VMEM((DEVICES, 2, WPLANES, S), BF16),
+            pltpu.VMEM((P_SIZE, WIDE), BF16),
+            pltpu.VMEM((8, F * ROWS, WIDE), BF16),
+            pltpu.VMEM((F * ROWS, P_SIZE), F32),
             pltpu.VMEM((WPLANES * S, 2 * S), BF16),
             pltpu.VMEM((WPLANES * 2 * S, 2 * S), BF16),
             pltpu.VMEM((2 * S, WPLANES * 2 * S), BF16),
@@ -480,10 +508,14 @@
             pltpu.VMEM((2, EXT, 2 * S), F32),
             pltpu.VMEM((EXT, 2 * S), BF16),
             pltpu.VMEM((EXT, 2 * S), BF16),
+            pltpu.VMEM((EXT, WIDE), F32),
+            pltpu.SMEM((SLOTS,), jnp.int32),
             pltpu.SemaphoreType.DMA((8,)),
             pltpu.SemaphoreType.DMA((CHUNKS,)),
-            pltpu.SemaphoreType.DMA((5,)),
-            pltpu.SemaphoreType.DMA((5,)),
+            pltpu.SemaphoreType.REGULAR,
+            pltpu.SemaphoreType.REGULAR,
+            pltpu.SemaphoreType.DMA((3,)),
+            pltpu.SemaphoreType.DMA((3,)),
             pltpu.SemaphoreType.DMA((3, F)),
             pltpu.SemaphoreType.DMA((3, F)),
         ],

time: 65.5 us -> 55.5 us (0.85)
  Pallas kernels: 63 us -> 53.1 us
    pallas_call x1, Pallas kernels: 63 us -> 53.1 us  [imaging(): pl.pallas_call(imaging_kernel, out_shape=jax.ShapeDtypeStruct((F * ROWS,...]
where the time goes in v4:
time: 55.5 us; the launch traced here: 55.3 us
  Pallas kernels  53.1 us (96%)
  local copies, waits for them, and re-layouts  1.57 us (3%)
  between operations  0.66 us (1%)
    pallas_call x1, Pallas kernels, imaging(): pl.pallas_call(imaging_kernel, out_shape=jax.ShapeDtypeStruct((F * ROWS,...  53.1 us
    unnamed x1, local copies, waits for them, and re-layouts  1.57 us

profile of v4, /device:TPU:0, one launch (start us, length us, event | category | flops | bytes accessed | tf_op | source)
XLA Modules:
  0.0 55.3 jit_solution(13677078139944423852)
XLA Ops:
  0.7 53.1 %imaging.1 = f32[64,512]{1,0:T(8,128)} custom-call(s32[32]{0:T(128)} %facet_hbm.1, s32[32]{0:T(128)} %patch_hbm.1, s32[32]{0:T(128)} %plane_hbm.1, s32[1]{0:T(128)S(6)} %copy.11.count_hbm, bf16[2,64,512]{2,1,0:T(8,128)(2,1)} %bitcast.3, bf16[2,512,512]{2,1,0:T(8,128)(2,1)} %constant.4.clone.cs_hbm, bf16[512,512]{1,0:T(8,128)(2,1)} %constant.5.clone.edge_hbm, ...), custom_call_target="tpu_custom_call" | custom-call | tf_op jit(solution)/shard_map/imaging/pallas_call | solution.py:474
  53.8 1.6 %copy.12 = f32[4,16,512]{2,1,0:T(8,128)} copy(f32[4,16,512]{2,1,0:T(8,128)} %bitcast.2) | data formatting | bytes 262144

commit v5 on v4

--- a/solution.py
+++ b/solution.py
@@ -72,12 +72,19 @@
     facet_ref, patch_ref, plane_ref, count_ref, sky_ref, cs_ref, edge_ref, w_ref, vis_buf,
     back_op, term_op, run_buf, grid_buf, to_rows, to_cols, half_buf, column_buf, u_buf, row_in,
     cnt_buf, left_op, right_op, b_buf, spread_buf,
-    first_out, first_in, second_out, second_in, third_own, third_out, third_in,
-    fold_buf, last_ref, load_sems, vis_sems, plane_sem, group_sem, send_sems, recv_sems, dirty_send, dirty_recv,
+    first_out, first_in, second_out, second_in,
+    fold_buf, last_ref, load_sems, vis_sems, send_sems, recv_sems, dirty_send, dirty_recv,
 ):
     me = lax.axis_index("vis")
     facet, row_block, column = owner(me)
     at_x, at_y, at_z = lax.rem(me, 4), lax.rem(lax.div(me, 4), 4), lax.div(me, 16)
+
+    barrier = pltpu.get_barrier_semaphore()
+
+    @pl.loop(1, DEVICES)
+    def _(k):
+        other = lax.rem(me + k, DEVICES)
+        pl.semaphore_signal(barrier, inc=1, device_id={"vis": other}, device_id_type=MESH)
 
     loads = [
         pltpu.make_async_copy(src, dst, load_sems.at[k])
@@ -96,20 +103,9 @@
         )
         for k in range(CHUNKS)
     ]
-    for copy in loads[:5] + vis_loads + loads[5:]:
+    for copy in loads[:4] + loads[5:] + loads[4:5] + vis_loads:
         copy.start()
 
-    barrier = pltpu.get_barrier_semaphore()
-
-    along_x = [at_z * 16 + at_y * 4 + lax.rem(at_x + k, 4) for k in range(1, 4)]
-    along_y = [at_z * 16 + lax.rem(at_y + k, 4) * 4 + at_x for k in range(1, 4)]
-    across = lax.rem(me + 16, DEVICES)
-
-    def tell(semaphore, others):
-        for other in others:
-            pl.semaphore_signal(semaphore, inc=1, device_id={"vis": other}, device_id_type=MESH)
-
-    tell(barrier, along_x + along_y + [across])
 
     def remote(src, dst, send, recv, other):
         return pltpu.make_async_remote_copy(
@@ -193,32 +189,6 @@
                 match = jnp.where(lane_row == 4 + k, in_slot[s:s + 1, :], match)
             cnt_buf[f * ROWS:(f + 1) * ROWS, c * S:(c + 1) * S] = contract(in_plane, match.astype(BF16), ((1,), (1,)))
 
-    loads[4].wait()
-
-    @pl.loop(0, WPLANES)
-    def _(w):
-        real, imag = w_ref[w, 0], w_ref[w, 1]
-        back_op[w] = lanes(real.T, imag.T)
-        term_op[w] = stack(lanes(real, -imag), lanes(imag, real))
-
-    run_buf[TILE_CAP] = jnp.zeros((S, 2 * S), F32)
-    for k in range(CHUNKS):
-        vis_loads[k].wait()
-        for t in range(k * VIS_CHUNK, (k + 1) * VIS_CHUNK):
-            plane = plane_ref[t]
-            real, imag = vis_buf[t, 0], vis_buf[t, 1]
-            half = dot(lanes(real, imag), term_op[plane])
-            half_real, half_imag = half[:, :S].astype(BF16), half[:, S:].astype(BF16)
-            term = dot(
-                back_op[plane], stack(lanes(half_real, half_imag), lanes(half_imag, -half_real))
-            )
-            run_buf[t] = term + run_buf[before[t, 0]]
-        if k == CHUNKS // 2 - 1:
-            pl.semaphore_wait(barrier, 7)
-            tell(plane_sem, along_y)
-    pl.semaphore_wait(plane_sem, 3)
-    tell(group_sem, [across])
-
     loads[5].wait()
     loads[7].wait()
     for c in range(4):
@@ -234,6 +204,30 @@
     for c in range(4):
         half_buf[0, :, c * WIDE + 2 * S:(c + 1) * WIDE] = extra[:, c * S:(c + 1) * S].astype(BF16)
 
+    loads[4].wait()
+
+    @pl.loop(0, WPLANES)
+    def _(w):
+        real, imag = w_ref[w, 0], w_ref[w, 1]
+        back_op[w] = lanes(real.T, imag.T)
+        term_op[w] = stack(lanes(real, -imag), lanes(imag, real))
+
+    run_buf[TILE_CAP] = jnp.zeros((S, 2 * S), F32)
+    for k in range(CHUNKS):
+        vis_loads[k].wait()
+        for t in range(k * VIS_CHUNK, (k + 1) * VIS_CHUNK):
+            plane = plane_ref[t]
+            real, imag = vis_buf[t, 0], vis_buf[t, 1]
+            half = dot(lanes(real, imag), term_op[plane])
+            half_real, half_imag = half[:, :S].astype(BF16), half[:, S:].astype(BF16)
+            term = dot(
+                back_op[plane], stack(lanes(half_real, half_imag), lanes(half_imag, -half_real))
+            )
+            run_buf[t] = term + run_buf[before[t, 0]]
+        if k == 6:
+            pl.semaphore_wait(barrier, DEVICES - 1)
+            exchange_columns(0)
+
     mirror_rows = where_equal(
         (S, 2 * S), lambda i, k: one_if(((k == S - i) & (i > 0)) | ((k == S) & (i == 0)))
     )
@@ -273,37 +267,25 @@
                 at_z * 16 + y * 4 + x,
             ).start()
 
-    def second_stage(group):
-        for f in (2 * group, 2 * group + 1):
-            wait_for(first_in.at[f], dirty_recv.at[0, f])
-            total = first_out[f, :, at_x if group == 0 else at_y].astype(F32)
-            for k in range(3):
-                total += first_in[f, k].astype(F32)
-            second_out[group, 2 * (f % 2):2 * (f % 2) + 2] = total.astype(BF16)
-        for k in range(1, 4):
-            if group == 0:
-                step = lax.rem(at_y + k, 4)
-                other = at_z * 16 + step * 4 + at_x
-            else:
-                step = lax.rem(at_x + k, 4)
-                other = at_z * 16 + at_y * 4 + step
-            remote(
-                second_out.at[group, step], second_in.at[group, k - 1],
-                dirty_send.at[1, group], dirty_recv.at[1, group], other,
-            ).start()
-
-    def third_sum(group):
-        wait_for(second_in.at[group], dirty_recv.at[1, group])
-        total = second_out[group, at_y if group == 0 else at_x].astype(F32)
+    def second_stage(f):
+        wait_for(first_in.at[f], dirty_recv.at[0, f])
+        turn, part = lax.div(f, 2), lax.rem(f, 2)
+        total = first_out[f, :, at_x + turn * (at_y - at_x)].astype(F32)
         for k in range(3):
-            total += second_in[group, k].astype(F32)
-        third_own[group] = total
-
-    def third_stage():
-        third_out[...] = third_own[1 - at_z].astype(BF16)
-        remote(
-            third_out, third_in, dirty_send.at[2, 0], dirty_recv.at[2, 0], lax.rem(me + 16, DEVICES)
-        ).start()
+            total += first_in[f, k].astype(F32)
+        second_out[f] = total.astype(BF16)
+        place = second_in.at[at_z * 4 + at_y + turn * (at_x - at_y)]
+        for r in range(2):
+            a = 2 * part + r
+            other = turn * 16 + (a + turn * (at_y - a)) * 4 + at_x + turn * (a - at_x)
+
+            @pl.when(other == me)
+            def _():
+                pltpu.make_async_copy(second_out.at[f, r], place, dirty_recv.at[1, 0]).start()
+
+            @pl.when(other != me)
+            def _():
+                remote(second_out.at[f, r], place, dirty_send.at[1, 0], dirty_recv.at[1, 0], other).start()
 
     def hermitian_rows(f, model=None):
         for s in range(NP):
@@ -345,12 +327,10 @@
 
     turn, part = lax.div(facet, 2), lax.rem(facet, 2)
     others = (2 * (1 - turn) + part, 2 * turn + 1 - part, 2 * (1 - turn) + 1 - part)
-    pl.semaphore_wait(group_sem, 1)
-    exchange_columns(0)
-    exchange_columns(1)
-    for f in others:
+    for f in others[:2]:
         hermitian_rows(f)
         first_stage(f)
+    hermitian_rows(others[2])
 
     @pl.loop(0, WPLANES)
     def _(w):
@@ -417,7 +397,9 @@
     model, folded_model = slot_model(model_grid(0).astype(BF16))
     fold_buf[...] = folded_model
     hermitian_rows(facet, model)
+    first_stage(others[2])
     first_stage(facet)
+    exchange_columns(1)
     row = lax.broadcasted_iota(jnp.int32, (S, P_SIZE), 0)
     for c in range(4):
         at, first, edge = c * WIDE, c * S, (c + 1) % 4 * S
@@ -428,15 +410,14 @@
         to_rows[at + 2 * S:at + WIDE, :] = jnp.where(
             row == 0, cosine_row, jnp.where(row == 1, -sine_row, 0.0)
         ).astype(BF16)
-    second_stage(0)
-    second_stage(1)
+    for f in others + (facet,):
+        second_stage(f)
     wait_for(column_buf.at[1, :, :, pl.ds(0, 2 * S)], recv_sems.at[2])
     grid = model_grid(1)
-    third_sum(0)
-    third_sum(1)
-    third_stage()
-    wait_for(third_in, dirty_recv.at[2, 0])
-    dirty = third_own[at_z] + third_in[...].astype(F32)
+    wait_for(second_in, dirty_recv.at[1, 0])
+    dirty = second_in[0].astype(F32)
+    for k in range(1, 8):
+        dirty += second_in[k].astype(F32)
     tail = dirty[S:].astype(BF16)
     ends = contract(tail[:, :S], put_real, ((0,), (0,))) + contract(tail[:, S:], put_imag, ((0,), (0,)))
     corner_row = lax.broadcasted_iota(jnp.int32, (ROWS, S), 0)
@@ -464,9 +445,7 @@
     wait_for(u_buf.at[pl.ds(0, P_SIZE - ROWS), :], send_sems.at[1])
     for f in range(F):
         wait_for(first_in.at[f], dirty_send.at[0, f])
-    for group in range(2):
-        wait_for(second_in.at[group], dirty_send.at[1, group])
-    wait_for(third_in, dirty_send.at[2, 0])
+    wait_for(second_in.at[pl.ds(0, 7)], dirty_send.at[1, 0])
 
 
 def imaging(*operands):
@@ -503,21 +482,16 @@
             pltpu.VMEM((2 * S, WIDE), BF16),
             pltpu.VMEM((F, 2, 4, EXT, 2 * S), BF16),
             pltpu.VMEM((F, 3, 2, EXT, 2 * S), BF16),
-            pltpu.VMEM((2, 4, EXT, 2 * S), BF16),
-            pltpu.VMEM((2, 3, EXT, 2 * S), BF16),
-            pltpu.VMEM((2, EXT, 2 * S), F32),
-            pltpu.VMEM((EXT, 2 * S), BF16),
-            pltpu.VMEM((EXT, 2 * S), BF16),
+            pltpu.VMEM((F, 2, EXT, 2 * S), BF16),
+            pltpu.VMEM((8, EXT, 2 * S), BF16),
             pltpu.VMEM((EXT, WIDE), F32),
             pltpu.SMEM((SLOTS,), jnp.int32),
             pltpu.SemaphoreType.DMA((8,)),
             pltpu.SemaphoreType.DMA((CHUNKS,)),
-            pltpu.SemaphoreType.REGULAR,
-            pltpu.SemaphoreType.REGULAR,
             pltpu.SemaphoreType.DMA((3,)),
             pltpu.SemaphoreType.DMA((3,)),
-            pltpu.SemaphoreType.DMA((3, F)),
-            pltpu.SemaphoreType.DMA((3, F)),
+            pltpu.SemaphoreType.DMA((2, F)),
+            pltpu.SemaphoreType.DMA((2, F)),
         ],
         compiler_params=pltpu.CompilerParams(
             collective_id=0, has_side_effects=True, vmem_limit_bytes=56 << 20

time: 55.5 us -> 53.4 us (0.962)
  Pallas kernels: 53.1 us -> 51 us
    pallas_call x1, Pallas kernels: 53.1 us -> 51 us  [imaging(): pl.pallas_call(imaging_kernel, out_shape=jax.ShapeDtypeStruct((F * ROWS,...]
where the time goes in v5:
time: 53.4 us; the launch traced here: 53.2 us
  Pallas kernels  51 us (96%)
  local copies, waits for them, and re-layouts  1.57 us (3%)
  between operations  0.66 us (1%)
    pallas_call x1, Pallas kernels, imaging(): pl.pallas_call(imaging_kernel, out_shape=jax.ShapeDtypeStruct((F * ROWS,...  51 us
    unnamed x1, local copies, waits for them, and re-layouts  1.57 us

profile of v5, /device:TPU:0, one launch (start us, length us, event | category | flops | bytes accessed | tf_op | source)
XLA Modules:
  0.0 53.2 jit_solution(2914660149484904218)
XLA Ops:
  0.7 51.0 %imaging.1 = f32[64,512]{1,0:T(8,128)} custom-call(s32[32]{0:T(128)} %facet_hbm.1, s32[32]{0:T(128)} %patch_hbm.1, s32[32]{0:T(128)} %plane_hbm.1, s32[1]{0:T(128)S(6)} %copy.11.count_hbm, bf16[2,64,512]{2,1,0:T(8,128)(2,1)} %bitcast.3, bf16[2,512,512]{2,1,0:T(8,128)(2,1)} %constant.4.clone.cs_hbm, bf16[512,512]{1,0:T(8,128)(2,1)} %constant.5.clone.edge_hbm, ...), custom_call_target="tpu_custom_call" | custom-call | tf_op jit(solution)/shard_map/imaging/pallas_call | solution.py:453
  51.6 1.6 %copy.12 = f32[4,16,512]{2,1,0:T(8,128)} copy(f32[4,16,512]{2,1,0:T(8,128)} %bitcast.2) | data formatting | bytes 262144

commit v6 on v5

--- a/solution.py
+++ b/solution.py
@@ -385,10 +385,14 @@
 
     def image_rows():
         wait_for(row_in, recv_sems.at[1])
-        parts = [
-            (row_in[2 * c].astype(F32) + row_in[2 * c + 1].astype(F32)).astype(BF16)
-            for c in range(4)
-        ]
+        parts = []
+        edge = jnp.zeros((F * ROWS, S), F32)
+        for c in range(4):
+            both = row_in[2 * c].astype(F32) + row_in[2 * c + 1].astype(F32)
+            parts.append(both[:, :2 * S].astype(BF16))
+            ends = both[:, 2 * S:]
+            edge += pltpu.roll(ends, 2 * c, 1) if c else ends
+        parts.append(edge.astype(BF16))
         return dot(lanes(*parts), to_rows[...])
 
     wait_for(column_buf.at[0], recv_sems.at[0])
@@ -401,15 +405,15 @@
     first_stage(facet)
     exchange_columns(1)
     row = lax.broadcasted_iota(jnp.int32, (S, P_SIZE), 0)
+    edge_rows = jnp.zeros((S, P_SIZE), F32)
     for c in range(4):
-        at, first, edge = c * WIDE, c * S, (c + 1) % 4 * S
+        at, first, edge = c * 2 * S, c * S, (c + 1) % 4 * S
         to_rows[at:at + S, :] = cs_ref[0, first:first + S, :]
         to_rows[at + S:at + 2 * S, :] = -cs_ref[1, first:first + S, :]
         cosine_row = cs_ref[0, edge:edge + 1, :].astype(F32)
         sine_row = cs_ref[1, edge:edge + 1, :].astype(F32)
-        to_rows[at + 2 * S:at + WIDE, :] = jnp.where(
-            row == 0, cosine_row, jnp.where(row == 1, -sine_row, 0.0)
-        ).astype(BF16)
+        edge_rows = jnp.where(row == 2 * c, cosine_row, jnp.where(row == 2 * c + 1, -sine_row, edge_rows))
+    to_rows[2 * P_SIZE:, :] = edge_rows.astype(BF16)
     for f in others + (facet,):
         second_stage(f)
     wait_for(column_buf.at[1, :, :, pl.ds(0, 2 * S)], recv_sems.at[2])
@@ -469,7 +473,7 @@
             pltpu.VMEM((WPLANES, 2 * S, 2 * S), BF16),
             pltpu.VMEM((TILE_CAP + 1, S, 2 * S), F32),
             pltpu.VMEM((NP, S, 2 * S), BF16),
-            pltpu.VMEM((4 * WIDE, P_SIZE), BF16),
+            pltpu.VMEM((2 * P_SIZE + S, P_SIZE), BF16),
             pltpu.VMEM((P_SIZE, 2 * P_SIZE), BF16),
             pltpu.VMEM((2, F * ROWS, 4 * WIDE), BF16),
             pltpu.VMEM((2, DEVICES, ROWS, WIDE), BF16),

time: 53.4 us -> 53.3 us (level)
  no operation moved by 1% of the time
where the time goes in v6:
time: 53.3 us; the launch traced here: 53.1 us
  Pallas kernels  50.8 us (95%)
  local copies, waits for them, and re-layouts  1.57 us (3%)
  between operations  0.66 us (1%)
    pallas_call x1, Pallas kernels, imaging(): pl.pallas_call(imaging_kernel, out_shape=jax.ShapeDtypeStruct((F * ROWS,...  50.8 us
    unnamed x1, local copies, waits for them, and re-layouts  1.57 us

profile of v6, /device:TPU:0, one launch (start us, length us, event | category | flops | bytes accessed | tf_op | source)
XLA Modules:
  0.0 53.1 jit_solution(9607015875293630626)
XLA Ops:
  0.7 50.8 %imaging.1 = f32[64,512]{1,0:T(8,128)} custom-call(s32[32]{0:T(128)} %facet_hbm.1, s32[32]{0:T(128)} %patch_hbm.1, s32[32]{0:T(128)} %plane_hbm.1, s32[1]{0:T(128)S(6)} %copy.11.count_hbm, bf16[2,64,512]{2,1,0:T(8,128)(2,1)} %bitcast.3, bf16[2,512,512]{2,1,0:T(8,128)(2,1)} %constant.4.clone.cs_hbm, bf16[512,512]{1,0:T(8,128)(2,1)} %constant.5.clone.edge_hbm, ...), custom_call_target="tpu_custom_call" | custom-call | tf_op jit(solution)/shard_map/imaging/pallas_call | solution.py:457
  51.5 1.6 %copy.12 = f32[4,16,512]{2,1,0:T(8,128)} copy(f32[4,16,512]{2,1,0:T(8,128)} %bitcast.2) | data formatting | bytes 262144
